TPU v7x, 32 devices: a whole 2x2x4 slice. The times are simulated.
32 devices in a mesh: dp: 4 (over y, x), fsdp: 8 (over z, core).
Axes of the slice: x: 2, y: 2, z: 4, core: 2. Of those that a mesh axis runs over, the one named last changes fastest.
Arguments:
- tokens: bfloat16 [12288, 8192], P(('dp', 'fsdp')), may hold values from -6 to 6
- frozen_value_weight: bfloat16 [8192, 1024], P('fsdp'), may hold values from -0.0625 to 0.0625
- adapter_down_weight: bfloat16 [32, 8192, 64], P('dp', 'fsdp'), may hold values from -0.0625 to 0.0625
- adapter_up_weight: bfloat16 [32, 64, 1024], P('dp', None, 'fsdp'), may hold values from -0.75 to 0.75
- output_gradient: bfloat16 [12288, 1024], P(('dp', 'fsdp')), may hold values from -6 to 6
- adapter_per_block: int32 [96], P(('dp', 'fsdp')), may hold values from 0 to 31, as said below
- block_live_count: int32 [96], P(('dp', 'fsdp')), may hold values from 1 to 128
Outputs:
- values: bfloat16 [12288, 1024], P(('dp', 'fsdp'))
- input_gradient: bfloat16 [12288, 8192], P(('dp', 'fsdp'))
- grad_down: float32 [32, 8192, 64], P('dp', 'fsdp')
- grad_up: float32 [32, 64, 1024], P('dp', None, 'fsdp')
Inputs may be any that keep to these rules, and one draw needn't show every extreme that they name: `adapter_per_block`: within the blocks of one device the adapter numbers never fall.
All inputs are finite; a program needn't handle non-finite values.
Results may differ from a plain program's by a relative error of at most 0.0038.
Values may be sent and summed in bfloat16 or wider, within the bound.
A program may use at most 192 MiB of HBM per device.

v0:
```python
import jax
import jax.numpy as jnp
from jax import lax
from jax.experimental import pallas as pl
from jax.experimental.pallas import tpu as pltpu
from jax.sharding import PartitionSpec as P

adapter_scale = 0.5
cores = 2


def spread(part, axis):
    size = lax.axis_size(axis)
    copies = jnp.broadcast_to(part[None], (size,) + part.shape)
    return lax.all_to_all(copies, axis, split_axis=0, concat_axis=0, tiled=True)


def gather_frozen(piece, first, second):
    dp, fsdp = lax.axis_size("dp"), lax.axis_size("fsdp")
    rows, width = piece.shape
    chips = fsdp // cores
    share_rows = rows // dp
    share = lax.dynamic_slice_in_dim(piece, lax.axis_index("dp") * share_rows, share_rows, 0)
    same_core = [[chip * cores + core for chip in range(chips)] for core in range(cores)]
    same_chip = [[chip * cores + core for core in range(cores)] for chip in range(chips)]
    shares = lax.all_gather(share, "fsdp", axis=0, axis_index_groups=same_core)
    shares, _ = lax.optimization_barrier((shares, first))
    half = lax.all_gather(shares, "dp", axis=0)
    half, _ = lax.optimization_barrier((half, second))
    return lax.all_gather(half, "fsdp", axis=0, axis_index_groups=same_chip)


def dot(left, right, left_dim, right_dim):
    return lax.dot_general(
        left, right, (((left_dim,), (right_dim,)), ((), ())), preferred_element_type=jnp.float32
    )


def low_rank_kernel(fill_ref, x_ref, dy_ref, pieces_ref, terms_ref, u_ref, v_ref, u_sum, v_sum):
    slices, per_dev, rank, _ = pieces_ref.shape
    block_rows, outputs = dy_ref.shape[2:]
    features = x_ref.shape[1] // slices
    u_sum[...] = jnp.zeros_like(u_sum)
    v_sum[...] = jnp.zeros_like(v_sum)

    def x_of(block, index):
        columns = pl.ds(pl.multiple_of(index * features, features), features)
        return x_ref[block * block_rows : (block + 1) * block_rows, columns]

    @pl.loop(0, slices)
    def _(index):
        for block in range(per_dev):
            u_sum[block] += dot(x_of(block, index), pieces_ref[index, block, :, :features], 1, 1)
            v_sum[block] += dot(dy_ref[index, block], pieces_ref[index, block, :, features:], 1, 1)

    rows = lax.broadcasted_iota(jnp.int32, (block_rows, rank), 0)
    for block in range(per_dev):
        live = (rows < fill_ref[block]).astype(jnp.float32)
        u_ref[block] = (u_sum[block] * live).astype(jnp.bfloat16)
        v_ref[block] = (v_sum[block] * live).astype(jnp.bfloat16)

    @pl.loop(0, slices)
    def _(index):
        for block in range(per_dev):
            down_term = dot(v_ref[block], x_of(block, index), 0, 0)
            up_term = dot(u_ref[block], dy_ref[index, block], 0, 0)
            terms_ref[index, block, :, :features] = down_term.astype(jnp.bfloat16)
            terms_ref[index, block, :, features:] = up_term.astype(jnp.bfloat16)


def low_rank(fill, x, dy, pieces):
    slices, per_dev, rank, _ = pieces.shape
    block_rows = x.shape[0] // per_dev
    low = jax.ShapeDtypeStruct((per_dev, block_rows, rank), jnp.bfloat16)
    vmem = pl.BlockSpec(memory_space=pltpu.VMEM)
    size = 2 * (x.size + dy.size + 2 * pieces.size)
    return pl.pallas_call(
        low_rank_kernel,
        out_shape=(jax.ShapeDtypeStruct(pieces.shape, jnp.bfloat16), low, low),
        in_specs=[pl.BlockSpec(memory_space=pltpu.SMEM), vmem, vmem, vmem],
        out_specs=(vmem, vmem, vmem),
        scratch_shapes=[pltpu.VMEM(low.shape, jnp.float32)] * 2,
        cost_estimate=pl.CostEstimate(
            flops=8 * x.size * rank, bytes_accessed=size, transcendentals=0
        ),
        name="low_rank",
    )(fill, x, dy, pieces)


def combine_kernel(ids_ref, terms_ref, out_ref, total):
    total[...] = jnp.zeros_like(total)

    @pl.loop(0, terms_ref.shape[0])
    def _(block):
        owner = ids_ref[block]
        total[owner] += terms_ref[block].astype(jnp.float32)

    out_ref[...] = total[...].astype(out_ref.dtype)


def combine(ids, terms, adapters):
    shape = (adapters,) + terms.shape[1:]
    vmem = pl.BlockSpec(memory_space=pltpu.VMEM)
    return pl.pallas_call(
        combine_kernel,
        out_shape=jax.ShapeDtypeStruct(shape, jnp.bfloat16),
        in_specs=[pl.BlockSpec(memory_space=pltpu.SMEM), vmem],
        out_specs=vmem,
        scratch_shapes=[pltpu.VMEM(shape, jnp.float32)],
        name="combine",
    )(ids, terms)


def base_kernel(x_ref, dy_ref, w_ref, pieces_ref, up_ref, u_ref, v_ref, y_ref, dx_ref, total):
    index = pl.program_id(0)
    per_dev, block_rows, _ = u_ref.shape
    features = x_ref.shape[1]
    frozen = w_ref[...].reshape(features, w_ref.shape[-1])
    product = dot(x_ref[...], frozen, 1, 0)

    @pl.when(index == 0)
    def _():
        total[...] = product

    @pl.when(index > 0)
    def _():
        total[...] += product

    base_grad = dot(dy_ref[...], frozen, 1, 1)
    for block in range(per_dev):
        rows = slice(block * block_rows, (block + 1) * block_rows)
        pulled = dot(v_ref[block], pieces_ref[0, block, :, :features], 1, 0)
        pulled = pulled.astype(jnp.bfloat16).astype(jnp.float32)
        dx_ref[rows, :] = (base_grad[rows, :] + adapter_scale * pulled).astype(dx_ref.dtype)

    @pl.when(index == pl.num_programs(0) - 1)
    def _():
        for block in range(per_dev):
            rows = slice(block * block_rows, (block + 1) * block_rows)
            lifted = dot(u_ref[block], up_ref[block], 1, 0)
            lifted = lifted.astype(jnp.bfloat16).astype(jnp.float32)
            y_ref[rows, :] = (total[rows, :] + adapter_scale * lifted).astype(y_ref.dtype)


def base(x, dy, gathered, pieces, up, low_u, low_v):
    slices, per_dev, rank, piece_width = pieces.shape
    count_dev, model_width = x.shape
    width = dy.shape[1]
    features = model_width // slices
    _, dp, _, share_rows, _ = gathered.shape

    def whole(array):
        return pl.BlockSpec(array.shape, lambda index: (0,) * array.ndim)

    tile = pl.BlockSpec((count_dev, features), lambda index: (0, index))
    return pl.pallas_call(
        base_kernel,
        grid=(slices,),
        out_shape=(
            jax.ShapeDtypeStruct(dy.shape, jnp.bfloat16),
            jax.ShapeDtypeStruct(x.shape, jnp.bfloat16),
        ),
        in_specs=[
            tile,
            whole(dy),
            pl.BlockSpec(
                (1, dp, 1, share_rows, width),
                lambda index: (index % cores, 0, index // cores, 0, 0),
            ),
            pl.BlockSpec((1, per_dev, rank, piece_width), lambda index: (index, 0, 0, 0)),
            whole(up),
            whole(low_u),
            whole(low_v),
        ],
        out_specs=(whole(dy), tile),
        scratch_shapes=[pltpu.VMEM(dy.shape, jnp.float32)],
        compiler_params=pltpu.CompilerParams(dimension_semantics=("arbitrary",)),
        cost_estimate=pl.CostEstimate(
            flops=4 * x.size * width,
            bytes_accessed=2 * (2 * x.size + model_width * width),
            transcendentals=0,
        ),
        name="base",
    )(x, dy, gathered, pieces, up, low_u, low_v)


def body(
    tokens,
    frozen_value_weight,
    adapter_down_weight,
    adapter_up_weight,
    output_gradient,
    adapter_per_block,
    block_live_count,
):
    dp, fsdp = lax.axis_size("dp"), lax.axis_size("fsdp")
    count_dev, model_width = tokens.shape
    value_width = output_gradient.shape[1]
    per_dev = adapter_per_block.shape[0]
    block_rows = count_dev // per_dev
    own, features, rank = adapter_down_weight.shape
    outputs = adapter_up_weight.shape[2]
    total = own * dp
    ids_all = lax.all_gather(adapter_per_block, "fsdp", axis=0, tiled=True)
    ids_all, down, up = lax.optimization_barrier(
        (ids_all, adapter_down_weight, adapter_up_weight)
    )
    pieces = jnp.concatenate([down.transpose(0, 2, 1), up], axis=2)
    catalog_pieces = spread(pieces, "dp").reshape(total, rank, features + outputs)
    chosen = catalog_pieces[ids_all].reshape(fsdp, per_dev, rank, features + outputs)
    arrived = lax.all_to_all(chosen, "fsdp", split_axis=0, concat_axis=0, tiled=True)
    up_blocks = arrived[..., features:].transpose(1, 2, 0, 3).reshape(per_dev, rank, value_width)
    dy_slices = output_gradient.reshape(per_dev, block_rows, fsdp, outputs).transpose(2, 0, 1, 3)
    terms, low_u, low_v = low_rank(block_live_count, tokens, dy_slices, arrived)
    terms = lax.all_to_all(terms, "fsdp", split_axis=0, concat_axis=0, tiled=True)
    terms = terms.reshape(fsdp * per_dev, rank, features + outputs)
    sums = combine(ids_all, terms, total).reshape(dp, own, rank, features + outputs)
    sums = lax.all_to_all(sums, "dp", split_axis=0, concat_axis=0, tiled=True)
    gathered = gather_frozen(frozen_value_weight, catalog_pieces, terms)
    values, input_gradient = base(
        tokens, output_gradient, gathered, arrived, up_blocks, low_u, low_v
    )
    sums, values, input_gradient = lax.optimization_barrier((sums, values, input_gradient))
    gradients = adapter_scale * jnp.sum(sums.astype(jnp.float32), axis=0)
    grad_down = gradients[..., :features].transpose(0, 2, 1)
    grad_up = gradients[..., features:]
    return values, input_gradient, grad_down, grad_up


def solution(mesh):
    placed = (
        P(("dp", "fsdp"), None),
        P("fsdp", None),
        P("dp", "fsdp", None),
        P("dp", None, "fsdp"),
        P(("dp", "fsdp"), None),
        P(("dp", "fsdp")),
        P(("dp", "fsdp")),
    )
    return jax.shard_map(
        body,
        mesh=mesh,
        in_specs=placed,
        out_specs=(
            P(("dp", "fsdp"), None),
            P(("dp", "fsdp"), None),
            P("dp", "fsdp", None),
            P("dp", None, "fsdp"),
        ),
        check_vma=False,
    )
```

profile of v0, /device:TPU:25, one launch (start us, length us, event | category | flops | bytes accessed | tf_op | source)
XLA Modules:
  0.0 340.4 jit_solution(10289707199115874506)
XLA Ops:
  7.2 0.0 copy-start
  7.2 1.4 dynamic-slice
  9.2 0.9 dynamic-update-slice
  10.1 4.2 %all-reduce.ids_ref = s32[24]{0:T(128)S(1)} all-reduce(s32[24]{0:T(128)S(1)} %dynamic-update-slice), channel_id=1, replica_groups=mesh['dp'=4,'fsdp'=8] {'fsdp'}, use_global_device_ids=true, to_apply=%add | all-reduce | flops 24 | bytes 192 | tf_op jit(solution)/shard_map/optimization_barrier | solution.py:205
  14.3 0.0 copy-start.3
  14.3 1.4 pad_maximum_fusion
  15.7 2.8 broadcast_in_dim.4
  18.5 5.0 %all-to-all-start = ((bf16[4,8,64,1152]{3,2,1,0:T(8,128)(2,1)}), bf16[4,8,64,1152]{3,2,1,0:T(8,128)(2,1)}, u32[]{:S(2)}, u32[]{:S(2)}) async-start(bf16[4,8,64,1152]{3,2,1,0:T(8,128)(2,1)} %broadcast_in_dim.4), calls=%async_computation | async-start | bytes 9437184 | tf_op jit(solution)/shard_map/all_to_all | solution.py:15
  23.5 0.0 all-gather.7.cloned.1.call-start
  23.6 0.0 copy-done
  23.6 0.8 constant_dynamic-slice_fusion
  24.4 0.0 all-gather.7.cloned.1.call-update
  24.4 0.0 all-gather.9.cloned.1.call-start
  24.5 0.0 copy-done.3
  24.5 49.5 %all-gather.7.cloned.1.call-done = bf16[1024,1024]{1,0:T(8,128)(2,1)} async-done(((bf16[256,1024]{1,0:T(8,128)(2,1)}), bf16[1024,1024]{1,0:T(8,128)(2,1)}) %all-gather.7.cloned.1.call-update) | async-done | bytes 2097168 | tf_op jit(solution)/shard_map/all_gather | solution.py:26
  74.0 2.0 all-to-all-done
  76.0 0.0 all-gather.9.cloned.1.call-update
  76.1 5.3 %gather_fusion = bf16[24,64,1152]{2,1,0:T(8,128)(2,1)} fusion(bf16[32,64,1152]{2,1,0:T(8,128)(2,1)} %bitcast.3, s32[1024]{0:T(1024)S(1)} %pad_clamp_fusion), kind=kCustom, calls=%fused_computation | custom fusion | bytes 7077984 | tf_op jit(solution)/shard_map/gather | solution.py:210
  81.4 0.0 copy-start.2
  81.4 9.5 %all-to-all-start.1 = ((bf16[8,3,64,1152]{3,2,1,0:T(8,128)(2,1)}), bf16[8,3,64,1152]{3,2,1,0:T(8,128)(2,1)}, u32[]{:S(2)}, u32[]{:S(2)}) async-start(bf16[8,3,64,1152]{3,2,1,0:T(8,128)(2,1)} %bitcast.24), calls=%async_computation.1 | async-start | bytes 7077888 | tf_op jit(solution)/shard_map/all_to_all | solution.py:211
  90.9 0.0 all-gather.11.cloned.1.call-start
  90.9 0.0 copy-done.2
  90.9 0.2 copy.17
  91.1 1.1 copy.20
  92.1 76.2 %all-to-all-done.1.pieces_ref = bf16[8,3,64,1152]{3,2,1,0:T(8,128)(2,1)} async-done(((bf16[8,3,64,1152]{3,2,1,0:T(8,128)(2,1)}), bf16[8,3,64,1152]{3,2,1,0:T(8,128)(2,1)}, u32[]{:S(2)}, u32[]{:S(2)}) %all-to-all-start.1) | async-done | bytes 3538976 | tf_op jit(solution)/shard_map/all_to_all | solution.py:211
  168.3 11.4 %low_rank.1 = (bf16[8,3,64,1152]{3,2,1,0:T(8,128)(2,1)}, bf16[3,128,64]{2,1,0:T(8,128)(2,1)}, bf16[3,128,64]{2,1,0:T(8,128)(2,1)}) custom-call(s32[3]{0:T(128)} %fill_ref.1, bf16[384,8192]{1,0:T(8,128)(2,1)} %x_ref.3, bf16[8,3,128,128]{3,2,1,0:T(8,128)(2,1)} %bitcast.28, bf16[8,3,64,1152]{3,2,1,0:T(8,128)(2,1)} %all-to-all-done.1.pieces_ref), custom_call_target="tpu_custom_call" | custom-call | flops 1610612736 | bytes 14155776 | tf_op jit(solution)/shard_map/low_rank/pallas_call | solution.py:77
  179.7 84.4 %all_to_all.20 = bf16[8,3,64,1152]{3,2,1,0:T(8,128)(2,1)} all-to-all(bf16[8,3,64,1152]{3,2,1,0:T(8,128)(2,1)} %get-tuple-element.20), channel_id=1, replica_groups=mesh['dp'=4,'fsdp'=8] {'fsdp'}, dimensions={0} | all-to-all | bytes 7077888 | tf_op jit(solution)/shard_map/all_to_all | solution.py:215
  264.1 0.0 all-gather.9.cloned.1.call-done
  264.1 0.0 all-gather.11.cloned.1.call-update
  264.1 6.0 %combine.1 = bf16[32,64,1152]{2,1,0:T(8,128)(2,1)} custom-call(s32[24]{0:T(128)} %copy-done.3, bf16[24,64,1152]{2,1,0:T(8,128)(2,1)} %bitcast.25), custom_call_target="tpu_custom_call" | custom-call | tf_op jit(solution)/shard_map/combine/pallas_call | solution.py:104
  270.1 5.2 %all-to-all-start.3 = ((bf16[4,8,64,1152]{3,2,1,0:T(8,128)(2,1)}), bf16[4,8,64,1152]{3,2,1,0:T(8,128)(2,1)}, u32[]{:S(2)}, u32[]{:S(2)}) async-start(bf16[4,8,64,1152]{3,2,1,0:T(8,128)(2,1)} %bitcast.23), calls=%async_computation.3 | async-start | bytes 9437184 | tf_op jit(solution)/shard_map/all_to_all | solution.py:218
  275.3 1.9 copy_bitcast_fusion.1.up_ref
  277.3 17.5 %all-gather.11.cloned.1.call-done = bf16[8,4,256,1024]{3,2,1,0:T(8,128)(2,1)} async-done(((bf16[4,4,256,1024]{3,2,1,0:T(8,128)(2,1)}), bf16[8,4,256,1024]{3,2,1,0:T(8,128)(2,1)}) %all-gather.11.cloned.1.call-update) | async-done | bytes 16777232 | tf_op jit(solution)/shard_map/all_gather | solution.py:30
  294.8 23.0 %base.1 = (bf16[384,1024]{1,0:T(8,128)(2,1)}, bf16[384,8192]{1,0:T(8,128)(2,1)}) custom-call(bf16[384,8192]{1,0:T(8,128)(2,1)} %x_ref.3, bf16[384,1024]{1,0:T(8,128)(2,1)} %dy_ref.1, bf16[2,4,4,256,1024]{4,3,2,1,0:T(8,128)(2,1)} %bitcast.32, bf16[8,3,64,1152]{3,2,1,0:T(8,128)(2,1)} %all-to-all-done.1.pieces_ref, ...), custom_call_target="tpu_custom_call" | custom-call | flops 12884901888 | bytes 29360128 | tf_op jit(solution)/shard_map/base/pallas_call | solution.py:156
  317.8 10.2 %all-to-all-done.3 = bf16[4,8,64,1152]{3,2,1,0:T(8,128)(2,1)} async-done(((bf16[4,8,64,1152]{3,2,1,0:T(8,128)(2,1)}), bf16[4,8,64,1152]{3,2,1,0:T(8,128)(2,1)}, u32[]{:S(2)}, u32[]{:S(2)}) %all-to-all-start.3) | async-done | bytes 4718624 | tf_op jit(solution)/shard_map/all_to_all | solution.py:218
  328.0 3.4 convert_reduce_fusion
  331.3 0.0 copy-start.1
  331.4 0.2 broadcast_multiply_fusion
  331.6 1.6 slice_bitcast_fusion
  333.2 0.7 slice.16
  333.9 0.0 copy-done.1
  (3 shorter events, 0.0 us)
Async XLA Ops:
  7.2 16.4 %copy-start = (bf16[1024,1024]{1,0:T(8,128)(2,1)S(1)}, bf16[1024,1024]{1,0:T(8,128)(2,1)}, u32[]{:S(2)}) copy-start(bf16[1024,1024]{1,0:T(8,128)(2,1)} %param.8) | copy-start | bytes 6291460
  14.3 10.2 %copy-start.3 = (s32[24]{0:T(128)}, s32[24]{0:T(128)S(1)}, u32[]{:S(2)}) copy-start(s32[24]{0:T(128)S(1)} %all-reduce.ids_ref) | copy-start | bytes 292
  18.5 57.5 %all-to-all-start = ((bf16[4,8,64,1152]{3,2,1,0:T(8,128)(2,1)}), bf16[4,8,64,1152]{3,2,1,0:T(8,128)(2,1)}, u32[]{:S(2)}, u32[]{:S(2)}) async-start(bf16[4,8,64,1152]{3,2,1,0:T(8,128)(2,1)} %broadcast_in_dim.4), calls=%async_computation | async-start | bytes 9437184 | tf_op jit(solution)/shard_map/all_to_all | solution.py:15
  23.5 50.5 %all-gather.7.cloned.1.call-start = ((), (), s32[]{:S(2)}) async-start(), calls=%async_computation.4 | async-start | bytes 2621440 | tf_op jit(solution)/shard_map/all_gather | solution.py:26
  24.4 239.7 %all-gather.9.cloned.1.call-start = ((), (), s32[]{:S(2)}) async-start(), calls=%async_computation.5 | async-start | bytes 10485760 | tf_op jit(solution)/shard_map/all_gather | solution.py:28
  81.4 9.5 %copy-start.2 = (bf16[384,1024]{1,0:T(8,128)(2,1)S(1)}, bf16[384,1024]{1,0:T(8,128)(2,1)}, u32[]{:S(2)}) copy-start(bf16[384,1024]{1,0:T(8,128)(2,1)} %dy_ref.1) | copy-start | bytes 2359300
  81.4 86.9 %all-to-all-start.1 = ((bf16[8,3,64,1152]{3,2,1,0:T(8,128)(2,1)}), bf16[8,3,64,1152]{3,2,1,0:T(8,128)(2,1)}, u32[]{:S(2)}, u32[]{:S(2)}) async-start(bf16[8,3,64,1152]{3,2,1,0:T(8,128)(2,1)} %bitcast.24), calls=%async_computation.1 | async-start | bytes 7077888 | tf_op jit(solution)/shard_map/all_to_all | solution.py:211
  90.9 203.9 %all-gather.11.cloned.1.call-start = ((), (), s32[]{:S(2)}) async-start(), calls=%async_computation.6 | async-start | bytes 25165824 | tf_op jit(solution)/shard_map/all_gather | solution.py:30
  270.1 57.9 %all-to-all-start.3 = ((bf16[4,8,64,1152]{3,2,1,0:T(8,128)(2,1)}), bf16[4,8,64,1152]{3,2,1,0:T(8,128)(2,1)}, u32[]{:S(2)}, u32[]{:S(2)}) async-start(bf16[4,8,64,1152]{3,2,1,0:T(8,128)(2,1)} %bitcast.23), calls=%async_computation.3 | async-start | bytes 9437184 | tf_op jit(solution)/shard_map/all_to_all | solution.py:218
  331.3 2.5 copy-start.1
Sparse Core Ops, SparseCore 0:
  26.5 47.5 all-gather.6
  76.2 88.4 all-gather.8
  264.2 30.4 all-gather.10
where the time goes:
time: 346 us; the launch traced here: 340 us
  waiting for transfers between devices  155 us (45%)
  blocking collectives  88.6 us (26%)
  Pallas kernels  40.4 us (12%)
  starting transfers between devices  19.8 us (6%)
  local copies, waits for them, and re-layouts  16.7 us (5%)
  between operations  14.5 us (4%)
  other arithmetic  4.98 us (1%)
    all_to_all x1, blocking collectives, body(): lax.all_to_all(terms, 'fsdp', split_axis=0, concat_axis=0, tiled=True)  84.4 us
    all_to_all x1, waiting for transfers between devices, body(): lax.all_to_all(chosen, 'fsdp', split_axis=0, concat_axis=0, tiled=True)  76.2 us
    all_gather x1, waiting for transfers between devices, gather_frozen(): shares = lax.all_gather(share, 'fsdp', axis=0, axis_index_groups=same_core)  49.5 us
    pallas_call x1, Pallas kernels, base(): pl.pallas_call(base_kernel, grid=(slices,), out_shape=(jax.ShapeDtypeStru...  23 us
    all_gather x1, waiting for transfers between devices, gather_frozen(): return lax.all_gather(half, 'fsdp', axis=0, axis_index_groups=same_chip)  17.5 us
    pallas_call x1, Pallas kernels, low_rank(): pl.pallas_call(low_rank_kernel, out_shape=(jax.ShapeDtypeStruct(pieces.sh...  11.4 us
    all_to_all x1, waiting for transfers between devices, body(): sums = lax.all_to_all(sums, 'dp', split_axis=0, concat_axis=0, tiled=True)  10.2 us
    all_to_all x1, starting transfers between devices, body(): lax.all_to_all(chosen, 'fsdp', split_axis=0, concat_axis=0, tiled=True)  9.5 us
  transfers between devices with their start and end apart: 6, of which 5 were waited for; matrix products, arithmetic and copies ran while one was open for 3% of the time, Pallas kernels for 12%

commit v1 on v0

v1 whole, which is shorter than its diff:
```python
import functools

import jax
import jax.numpy as jnp
from jax import lax
from jax.experimental import pallas as pl
from jax.experimental.pallas import tpu as pltpu
from jax.sharding import PartitionSpec as P

adapter_scale = 0.5
cores = 2
rows_chunk = 16
mesh_ids = pl.DeviceIdType.MESH


def dot(left, right, left_dim, right_dim):
    return lax.dot_general(
        left, right, (((left_dim,), (right_dim,)), ((), ())), preferred_element_type=jnp.float32
    )


def partner(position, offset, size):
    if size & (size - 1):
        return lax.rem(position + offset, size)
    bit = 1
    while bit < size:
        if offset & bit:
            position = position + bit - 2 * bit * lax.rem(position // bit, 2)
        bit *= 2
    return position


def kernel(
    dp, fsdp,
    ids_ref, fill_ref, pieces_ref, w_ref, x_hbm, dy_hbm,
    y_out, dx_out, down_out, up_out,
    x, dy, dy_slices, catalog, outgoing, arrived, returned, sums_in, frozen, id_rows,
    pick, put, u_rows, v_rows, u_cols, v_cols, up_blocks, total, dx_tiles, y_tile, down_tile, up_tile,
    load_sem, own_sem, s1_send, s1_recv, id_send, id_recv, p_send, p_recv, t_send, t_recv,
    g_send, g_recv, right_send, right_recv, left_send, left_recv, w2_send, w2_recv, w3_send, w3_recv,
    dx_sem, out_sem,
):
    my_dp, me = lax.axis_index("dp"), lax.axis_index("fsdp")
    chunks, _, own_rows, piece_width = catalog.shape
    per_dev, rank_rows, block_rows = u_rows.shape[1:]
    count_dev, model_width = x.shape
    width = dy.shape[1]
    features, outputs = model_width // fsdp, width // fsdp
    block_group = per_dev * rank_rows
    lanes = fsdp * block_group
    total_rows = dp * own_rows
    own = own_rows // rank_rows
    chips = fsdp // cores
    chip, core = me // cores, lax.rem(me, cores)
    tile_lanes = 384 if piece_width % 384 == 0 else piece_width

    def peer(offset):
        return lax.rem(me + offset, fsdp)

    def column(slice_index):
        return pl.ds(pl.multiple_of(slice_index * features, features), features)

    loads = [
        pltpu.make_async_copy(x_hbm, x, load_sem.at[0]),
        pltpu.make_async_copy(dy_hbm, dy, load_sem.at[1]),
        pltpu.make_async_copy(w_ref, frozen.at[me], load_sem.at[2]),
    ]
    owns = [
        pltpu.make_async_copy(pieces_ref.at[k], catalog.at[k, my_dp], own_sem.at[k])
        for k in range(chunks)
    ]

    lane_block = lax.shift_right_logical(
        lax.broadcasted_iota(jnp.int32, (8, lanes), 1), rank_rows.bit_length() - 1
    )
    mine = jnp.zeros((8, lanes), jnp.int32)
    for block in range(per_dev):
        mine = jnp.where(lane_block == me * per_dev + block, ids_ref[block] + 1, mine)
    id_rows[me] = mine

    barrier = pltpu.get_barrier_semaphore()

    @pl.loop(1, fsdp)
    def _(offset):
        pl.semaphore_signal(barrier, inc=1, device_id=(my_dp, peer(offset)), device_id_type=mesh_ids)

    for offset in range(1, dp):
        pl.semaphore_signal(
            barrier, inc=1, device_id=(partner(my_dp, offset, dp), me), device_id_type=mesh_ids
        )
    pl.semaphore_wait(barrier, fsdp + dp - 2)

    def remote(source, target, send, recv, device):
        return pltpu.make_async_remote_copy(
            src_ref=source, dst_ref=target, send_sem=send, recv_sem=recv,
            device_id=device, device_id_type=mesh_ids,
        )

    def id_copy(offset):
        return remote(
            id_rows.at[me], id_rows.at[me], id_send.at[offset], id_recv.at[offset],
            (my_dp, peer(offset)),
        )

    def s1_copy(k, offset):
        return remote(
            pieces_ref.at[k], catalog.at[k, my_dp], s1_send.at[k, offset], s1_recv.at[k, offset],
            (partner(my_dp, offset, dp), me),
        )

    def p_copy(k, offset):
        return remote(
            outgoing.at[k, peer(offset)], arrived.at[k, me], p_send.at[k, offset],
            p_recv.at[k, offset], (my_dp, peer(offset)),
        )

    def t_copy(k, offset):
        return remote(
            outgoing.at[k, peer(offset)], returned.at[k, me], t_send.at[k, offset],
            t_recv.at[k, offset], (my_dp, peer(offset)),
        )

    def g_copy(k, offset):
        other = partner(my_dp, offset, dp)
        return remote(
            catalog.at[k, other], sums_in.at[k, my_dp], g_send.at[k, offset], g_recv.at[k, offset],
            (other, me),
        )

    def right_copy(step):
        source = w_ref.at[my_dp] if step == 0 else frozen.at[me - cores * step, my_dp]
        return remote(
            source, frozen.at[me - cores * step, my_dp], right_send.at[step], right_recv.at[step],
            (my_dp, me + cores),
        )

    def left_copy(step):
        source = w_ref.at[my_dp] if step == 0 else frozen.at[me + cores * step, my_dp]
        return remote(
            source, frozen.at[me + cores * step, my_dp], left_send.at[step], left_recv.at[step],
            (my_dp, me - cores),
        )

    def sends_right(step):
        return (chip >= step) & (chip + 1 < chips)

    def sends_left(step):
        return (chip + step < chips) & (chip >= 1)

    def gets_right(step):
        return chip >= step + 1

    def gets_left(step):
        return chip + step + 1 < chips

    def w2_copy(from_chip, offset):
        row = from_chip * cores + core
        return remote(
            frozen.at[row, my_dp], frozen.at[row, my_dp], w2_send.at[from_chip, offset],
            w2_recv.at[from_chip, offset], (partner(my_dp, offset, dp), me),
        )

    def w3_copy(from_chip):
        row = from_chip * cores + core
        return remote(
            frozen.at[row], frozen.at[row], w3_send.at[from_chip], w3_recv.at[from_chip],
            (my_dp, me + 1 - 2 * core),
        )

    def relay(step):
        @pl.when(gets_right(step))
        def _():
            right_copy(step).wait_recv()

        @pl.when(gets_left(step))
        def _():
            left_copy(step).wait_recv()

        if step + 1 < chips - 1:

            @pl.when(sends_right(step + 1))
            def _():
                right_copy(step + 1).start()

            @pl.when(sends_left(step + 1))
            def _():
                left_copy(step + 1).start()

    def spread_shares(step):
        @pl.when(gets_right(step))
        def _():
            for offset in range(1, dp):
                w2_copy(chip - step - 1, offset).start()

        @pl.when(gets_left(step))
        def _():
            for offset in range(1, dp):
                w2_copy(chip + step + 1, offset).start()

    @pl.loop(1, fsdp)
    def _(offset):
        id_copy(offset).start()

    for offset in range(1, dp):
        s1_copy(0, offset).start()

    @pl.when(sends_right(0))
    def _():
        right_copy(0).start()

    @pl.when(sends_left(0))
    def _():
        left_copy(0).start()

    for k in range(1, chunks):
        for offset in range(1, dp):
            s1_copy(k, offset).start()
    for copy in owns + loads:
        copy.start()

    @pl.loop(1, fsdp)
    def _(offset):
        id_copy(offset).wait_recv()

    numbers = id_rows[0]
    for position in range(1, fsdp):
        numbers = numbers + id_rows[position]
    numbers = numbers[0:1, :] - 1
    shift = rank_rows.bit_length() - 1
    row = lax.broadcasted_iota(jnp.int32, (total_rows, lanes), 0)
    lane = lax.broadcasted_iota(jnp.int32, (total_rows, lanes), 1)
    same_rank = (row & (rank_rows - 1)) == (lane & (rank_rows - 1))
    same_adapter = lax.shift_right_logical(row, shift) == numbers
    hot = jnp.where(same_rank & same_adapter, 1.0, 0.0)
    put[...] = hot.astype(jnp.bfloat16)
    pick[...] = hot.T.astype(jnp.bfloat16)

    def choose(k):
        owns[k].wait()
        for offset in range(1, dp):
            s1_copy(k, offset).wait_recv()
        for start in range(0, piece_width, tile_lanes):
            table = catalog[k, :, :, start : start + tile_lanes].reshape(total_rows, tile_lanes)
            chosen = dot(pick[...], table, 1, 0).astype(jnp.bfloat16)
            outgoing[k, :, :, start : start + tile_lanes] = chosen.reshape(
                fsdp, block_group, tile_lanes
            )
        arrived[k, me] = outgoing[k, me]

        @pl.loop(1, fsdp)
        def _(offset):
            p_copy(k, offset).start()

    def low_rank(k):
        @pl.loop(1, fsdp)
        def _(offset):
            p_copy(k, offset).wait_recv()

        zero = jnp.zeros((rank_rows, block_rows), jnp.float32)

        def gather_low(index, sums):
            result = []
            for block in range(per_dev):
                tokens = slice(block * block_rows, (block + 1) * block_rows)
                ranks = slice(block * rank_rows, (block + 1) * rank_rows)
                u = dot(arrived[k, index, ranks, :features], x[tokens, column(index)], 1, 1)
                v = dot(arrived[k, index, ranks, features:], dy_slices[index, tokens, :], 1, 1)
                result += [sums[2 * block] + u, sums[2 * block + 1] + v]
            return tuple(result)

        sums = lax.fori_loop(0, fsdp, gather_low, (zero,) * (2 * per_dev))
        token = lax.broadcasted_iota(jnp.int32, (rank_rows, block_rows), 1)
        for block in range(per_dev):
            live = (token < fill_ref[block]).astype(jnp.float32)
            u_rows[k, block] = (sums[2 * block] * live).astype(jnp.bfloat16)
            v_rows[k, block] = (sums[2 * block + 1] * live).astype(jnp.bfloat16)

        def terms_of(index):
            for block in range(per_dev):
                tokens = slice(block * block_rows, (block + 1) * block_rows)
                ranks = slice(block * rank_rows, (block + 1) * rank_rows)
                down = dot(v_rows[k, block], x[tokens, column(index)], 1, 0)
                up = dot(u_rows[k, block], dy_slices[index, tokens, :], 1, 0)
                outgoing[k, index, ranks, :features] = down.astype(jnp.bfloat16)
                outgoing[k, index, ranks, features:] = up.astype(jnp.bfloat16)

        @pl.loop(1, fsdp)
        def _(offset):
            p_copy(k, offset).wait_send()

        @pl.loop(1, fsdp)
        def _(offset):
            terms_of(peer(offset))

            @pl.when(offset > 1)
            def _():
                t_copy(k, offset - 1).start()

        terms_of(me)
        t_copy(k, fsdp - 1).start()
        returned[k, me] = outgoing[k, me]

    def combine(k):
        @pl.loop(1, fsdp)
        def _(offset):
            t_copy(k, offset).wait_recv()

        for start in range(0, piece_width, tile_lanes):
            terms = returned[k, :, :, start : start + tile_lanes].reshape(lanes, tile_lanes)
            added = dot(put[...], terms, 1, 0).astype(jnp.bfloat16)
            catalog[k, :, :, start : start + tile_lanes] = added.reshape(dp, own_rows, tile_lanes)
        for offset in range(1, dp):
            g_copy(k, offset).start()
        sums_in[k, my_dp] = catalog[k, my_dp]

    def out_copies(k):
        part = pl.ds(k * rank_rows, rank_rows)
        return (
            pltpu.make_async_copy(down_tile.at[k], down_out.at[:, part, :], out_sem.at[0, k]),
            pltpu.make_async_copy(up_tile.at[k], up_out.at[:, part, :], out_sem.at[1, k]),
        )

    def finish(k):
        for offset in range(1, dp):
            g_copy(k, offset).wait_recv()
        added = sums_in[k, 0].astype(jnp.float32)
        for position in range(1, dp):
            added = added + sums_in[k, position].astype(jnp.float32)
        added = adapter_scale * added
        down_tile[k] = added[:, :features].reshape(own, rank_rows, features)
        up_tile[k] = added[:, features:].reshape(own, rank_rows, outputs)
        for copy in out_copies(k):
            copy.start()

    def columns_of_low():
        for block in range(per_dev):
            for rows, columns in ((u_rows, u_cols), (v_rows, v_cols)):
                whole = jnp.concatenate([rows[k, block] for k in range(chunks)], axis=0)
                columns[block] = whole.astype(jnp.float32).T.astype(jnp.bfloat16)
            for index in range(fsdp):
                part = slice(index * outputs, (index + 1) * outputs)
                ranks = slice(block * rank_rows, (block + 1) * rank_rows)
                for k in range(chunks):
                    up_blocks[block, k * rank_rows : (k + 1) * rank_rows, part] = arrived[
                        k, index, ranks, features:
                    ]

    def dx_copy(index):
        slot = lax.rem(index, 2)
        return pltpu.make_async_copy(dx_tiles.at[slot], dx_out.at[:, column(index)], dx_sem.at[slot])

    def base(first, last):
        @pl.loop(first, last)
        def _(index):
            weight = frozen[index].reshape(features, width)
            product = dot(x[:, column(index)], weight, 1, 0)

            @pl.when(index == 0)
            def _():
                total[...] = product

            @pl.when(index > 0)
            def _():
                total[...] += product

            base_grad = dot(dy[...], weight, 1, 1)

            @pl.when(index >= 2)
            def _():
                dx_copy(index - 2).wait()

            slot = lax.rem(index, 2)
            for block in range(per_dev):
                tokens = slice(block * block_rows, (block + 1) * block_rows)
                ranks = slice(block * rank_rows, (block + 1) * rank_rows)
                down = jnp.concatenate(
                    [arrived[k, index, ranks, :features] for k in range(chunks)], axis=0
                )
                pulled = dot(v_cols[block], down, 1, 0).astype(jnp.bfloat16).astype(jnp.float32)
                dx_tiles[slot, tokens, :] = (base_grad[tokens, :] + adapter_scale * pulled).astype(
                    jnp.bfloat16
                )
            dx_copy(index).start()

    y_copy = pltpu.make_async_copy(y_tile, y_out, load_sem.at[0])

    def last_values():
        for block in range(per_dev):
            tokens = slice(block * block_rows, (block + 1) * block_rows)
            lifted = dot(u_cols[block], up_blocks[block], 1, 0)
            lifted = lifted.astype(jnp.bfloat16).astype(jnp.float32)
            y_tile[tokens, :] = (total[tokens, :] + adapter_scale * lifted).astype(jnp.bfloat16)
        y_copy.start()

    hops = chips - 1
    relayed = 0
    choose(0)
    relay(0)
    choose(1)
    for copy in loads:
        copy.wait()
    for index in range(fsdp):
        dy_slices[index] = dy[:, index * outputs : (index + 1) * outputs]
    for k in range(2, chunks):
        choose(k)
    spread_shares(0)
    low_rank(0)
    for step in range(1, hops):
        relay(step)
        spread_shares(step)
    for k in range(1, chunks):
        low_rank(k)
        if k >= 2:
            combine(k - 2)
    columns_of_low()

    def w2_done(from_chip):
        @pl.when(from_chip != chip)
        def _():
            for offset in range(1, dp):
                w2_copy(from_chip, offset).wait_recv()

    for from_chip in range(chips):
        w2_done(from_chip)
        w3_copy(from_chip).start()
    for from_chip in range(chips):
        w3_copy(from_chip).wait_recv()
    base(0, fsdp // 2)
    combine(chunks - 2)
    base(fsdp // 2, fsdp)
    last_values()
    for k in range(chunks - 2):
        finish(k)
    combine(chunks - 1)
    finish(chunks - 2)
    finish(chunks - 1)

    @pl.loop(1, fsdp)
    def _(offset):
        id_copy(offset).wait_send()
        for k in range(chunks):
            t_copy(k, offset).wait_send()

    for k in range(chunks):
        for offset in range(1, dp):
            s1_copy(k, offset).wait_send()
            g_copy(k, offset).wait_send()
        for copy in out_copies(k):
            copy.wait()
    for step in range(hops):

        @pl.when(sends_right(step))
        def _():
            right_copy(step).wait_send()

        @pl.when(sends_left(step))
        def _():
            left_copy(step).wait_send()

    for from_chip in range(chips):

        @pl.when(from_chip != chip)
        def _():
            for offset in range(1, dp):
                w2_copy(from_chip, offset).wait_send()

        w3_copy(from_chip).wait_send()
    for index in (fsdp - 2, fsdp - 1):
        dx_copy(index).wait()
    y_copy.wait()


def body(
    tokens,
    frozen_value_weight,
    adapter_down_weight,
    adapter_up_weight,
    output_gradient,
    adapter_per_block,
    block_live_count,
):
    dp, fsdp = lax.axis_size("dp"), lax.axis_size("fsdp")
    count_dev, model_width = tokens.shape
    width = output_gradient.shape[1]
    per_dev = adapter_per_block.shape[0]
    block_rows = count_dev // per_dev
    own, features, rank = adapter_down_weight.shape
    outputs = adapter_up_weight.shape[2]
    piece_width = features + outputs
    chunks = rank // rows_chunk
    chips = fsdp // cores
    share_rows = frozen_value_weight.shape[0] // dp
    pieces = jnp.concatenate([adapter_down_weight.transpose(0, 2, 1), adapter_up_weight], axis=2)
    pieces = pieces.reshape(own, chunks, rows_chunk, piece_width).transpose(1, 0, 2, 3)
    pieces = pieces.reshape(chunks, own * rows_chunk, piece_width)
    weight = frozen_value_weight.reshape(dp, share_rows, width)
    block_group = per_dev * rows_chunk
    lanes = fsdp * block_group
    total_rows = dp * own * rows_chunk
    bf16, f32 = jnp.bfloat16, jnp.float32
    anywhere = pl.BlockSpec(memory_space=pl.ANY)
    scalars = pl.BlockSpec(memory_space=pltpu.SMEM)
    dma = pltpu.SemaphoreType.DMA
    scratch = [
        pltpu.VMEM((count_dev, model_width), bf16),
        pltpu.VMEM((count_dev, width), bf16),
        pltpu.VMEM((fsdp, count_dev, outputs), bf16),
        pltpu.VMEM((chunks, dp, own * rows_chunk, piece_width), bf16),
        pltpu.VMEM((chunks, fsdp, block_group, piece_width), bf16),
        pltpu.VMEM((chunks, fsdp, block_group, piece_width), bf16),
        pltpu.VMEM((chunks, fsdp, block_group, piece_width), bf16),
        pltpu.VMEM((chunks, dp, own * rows_chunk, piece_width), bf16),
        pltpu.VMEM((fsdp, dp, share_rows, width), bf16),
        pltpu.VMEM((fsdp, 8, lanes), jnp.int32),
        pltpu.VMEM((lanes, total_rows), bf16),
        pltpu.VMEM((total_rows, lanes), bf16),
        pltpu.VMEM((chunks, per_dev, rows_chunk, block_rows), bf16),
        pltpu.VMEM((chunks, per_dev, rows_chunk, block_rows), bf16),
        pltpu.VMEM((per_dev, block_rows, rank), bf16),
        pltpu.VMEM((per_dev, block_rows, rank), bf16),
        pltpu.VMEM((per_dev, rank, width), bf16),
        pltpu.VMEM((count_dev, width), f32),
        pltpu.VMEM((2, count_dev, features), bf16),
        pltpu.VMEM((count_dev, width), bf16),
        pltpu.VMEM((chunks, own, rows_chunk, features), f32),
        pltpu.VMEM((chunks, own, rows_chunk, outputs), f32),
        dma((3,)),
        dma((chunks,)),
        dma((chunks, dp)), dma((chunks, dp)),
        dma((fsdp,)), dma((fsdp,)),
        dma((chunks, fsdp)), dma((chunks, fsdp)),
        dma((chunks, fsdp)), dma((chunks, fsdp)),
        dma((chunks, dp)), dma((chunks, dp)),
        dma((chips,)), dma((chips,)),
        dma((chips,)), dma((chips,)),
        dma((chips, dp)), dma((chips, dp)),
        dma((chips,)), dma((chips,)),
        dma((2,)),
        dma((2, chunks)),
    ]
    values, input_gradient, grad_down, grad_up = pl.pallas_call(
        functools.partial(kernel, dp, fsdp),
        out_shape=(
            jax.ShapeDtypeStruct((count_dev, width), bf16),
            jax.ShapeDtypeStruct((count_dev, model_width), bf16),
            jax.ShapeDtypeStruct((own, rank, features), f32),
            jax.ShapeDtypeStruct((own, rank, outputs), f32),
        ),
        in_specs=[scalars, scalars] + [anywhere] * 4,
        out_specs=(anywhere,) * 4,
        scratch_shapes=scratch,
        compiler_params=pltpu.CompilerParams(
            collective_id=0, has_side_effects=True, vmem_limit_bytes=66_000_000
        ),
        name="lora",
    )(adapter_per_block, block_live_count, pieces, weight, tokens, output_gradient)
    return values, input_gradient, grad_down.transpose(0, 2, 1), grad_up


def solution(mesh):
    placed = (
        P(("dp", "fsdp"), None),
        P("fsdp", None),
        P("dp", "fsdp", None),
        P("dp", None, "fsdp"),
        P(("dp", "fsdp"), None),
        P(("dp", "fsdp")),
        P(("dp", "fsdp")),
    )
    return jax.shard_map(
        body,
        mesh=mesh,
        in_specs=placed,
        out_specs=(
            P(("dp", "fsdp"), None),
            P(("dp", "fsdp"), None),
            P("dp", "fsdp", None),
            P("dp", None, "fsdp"),
        ),
        check_vma=False,
    )
```

time: 346 us -> 234 us (0.68); the launches traced: 340 us -> 232 us
  Pallas kernels: 40.4 us -> 219 us
  waiting for transfers between devices: 155 us -> 0 us
  blocking collectives: 88.6 us -> 0 us
  starting transfers between devices: 19.8 us -> 0 us
  between operations: 14.5 us -> 0.65 us
  local copies, waits for them, and re-layouts: 16.7 us -> 11.5 us
  other arithmetic: 4.98 us -> 1.42 us
    pallas_call x3 -> x1, Pallas kernels: 40.4 us -> 219 us  [body(): pl.pallas_call(functools.partial(kernel, dp, fsdp), out_shape=(jax.ShapeD...]
    all_to_all x3 -> x0, waiting for transfers between devices: 88.4 us -> none  [the longest x1 76.2 us: body(): lax.all_to_all(chosen, 'fsdp', split_axis=0, concat_axis=0, tiled=True)]
    all_to_all x1 -> x0, blocking collectives: 84.4 us -> none  [body(): lax.all_to_all(terms, 'fsdp', split_axis=0, concat_axis=0, tiled=True)]
    all_gather x3 -> x0, waiting for transfers between devices: 67 us -> none  [the longest x1 49.5 us: gather_frozen(): shares = lax.all_gather(share, 'fsdp', axis=0, axis_index_groups=same_core)]
    all_to_all x3 -> x0, starting transfers between devices: 19.7 us -> none  [the longest x1 9.5 us: body(): lax.all_to_all(chosen, 'fsdp', split_axis=0, concat_axis=0, tiled=True)]
    unnamed x12 -> x8, local copies, waits for them, and re-layouts: 2.44 us -> 10.4 us
    gather x1 -> x0, local copies, waits for them, and re-layouts: 5.28 us -> none  [body(): catalog_pieces[ids_all].reshape(fsdp, per_dev, rank, features + outputs)]
    optimization_barrier x1 -> x0, blocking collectives: 4.18 us -> none  [body(): lax.optimization_barrier((ids_all, adapter_down_weight, adapter_up_weight))]
  transfers between devices with their start and end apart: 6 -> 0, of which waited for: 5 -> 0; matrix products, arithmetic and copies ran while one was open for 3% -> 0% of each run, Pallas kernels for 12% -> 0%
where the time goes in v1:
time: 234 us; the launch traced here: 232 us
  Pallas kernels  219 us (94%)
  local copies, waits for them, and re-layouts  11.5 us (5%)
    pallas_call x1, Pallas kernels, body(): pl.pallas_call(functools.partial(kernel, dp, fsdp), out_shape=(jax.ShapeD...  219 us
    unnamed x8, local copies, waits for them, and re-layouts  10.4 us

profile of v1, /device:TPU:25, one launch (start us, length us, event | category | flops | bytes accessed | tf_op | source)
XLA Modules:
  0.0 232.4 jit_solution(14373635187139942707)
XLA Ops:
  0.6 1.4 pad_maximum_fusion
  2.1 1.1 copy.11
  3.2 218.8 %lora.1 = (bf16[384,1024]{1,0:T(8,128)(2,1)}, bf16[384,8192]{1,0:T(8,128)(2,1)}, f32[8,64,1024]{2,1,0:T(8,128)}, f32[8,64,128]{2,1,0:T(8,128)}) custom-call(s32[3]{0:T(128)} %ids_ref.1, s32[3]{0:T(128)} %fill_ref.1, bf16[4,128,1152]{2,1,0:T(8,128)(2,1)} %bitcast.8, bf16[4,256,1024]{2,1,0:T(8,128)(2,1)} %bitcast.10, bf16[384,8192]{1,0:T(8,128)(2,1)} %x_hbm.1, ...), custom_call_target="tpu_custom_call" | custom-call | tf_op jit(solution)/shard_map/lora/pallas_call | solution.py:541
  221.9 2.1 copy.16
  224.0 0.0 copy-start
  224.0 6.3 %copy.17 = bf16[384,8192]{1,0:T(8,128)(2,1)} copy(bf16[384,8192]{1,0:T(8,128)(2,1)} %get-tuple-element.17) | data formatting | bytes 12582912
  230.3 0.0 copy-done
  230.3 0.0 copy-start.1
  230.3 1.3 copy.18
  231.7 0.0 copy-done.1
  231.7 0.7 copy.19
Async XLA Ops:
  224.0 6.3 %copy-start = (f32[8,64,1024]{2,1,0:T(8,128)S(1)}, f32[8,64,1024]{2,1,0:T(8,128)}, u32[]{:S(2)}) copy-start(f32[8,64,1024]{2,1,0:T(8,128)} %get-tuple-element.10) | copy-start | bytes 6291460
  230.3 1.3 copy-start.1

commit v2 on v1

--- a/solution.py
+++ b/solution.py
@@ -30,29 +30,33 @@
     return position
 
 
+def lane_tile(piece_width):
+    return 384 if piece_width % 384 == 0 else piece_width
+
+
 def kernel(
     dp, fsdp,
-    ids_ref, fill_ref, pieces_ref, w_ref, x_hbm, dy_hbm,
+    ids_ref, fill_ref, down_ref, up_ref, w_ref, x_hbm, dy_hbm,
     y_out, dx_out, down_out, up_out,
     x, dy, dy_slices, catalog, outgoing, arrived, returned, sums_in, frozen, id_rows,
-    pick, put, u_rows, v_rows, u_cols, v_cols, up_blocks, total, dx_tiles, y_tile, down_tile, up_tile,
+    pick, put, u_rows, v_rows, u_cols, v_cols, up_blocks, total,
     load_sem, own_sem, s1_send, s1_recv, id_send, id_recv, p_send, p_recv, t_send, t_recv,
     g_send, g_recv, right_send, right_recv, left_send, left_recv, w2_send, w2_recv, w3_send, w3_recv,
-    dx_sem, out_sem,
 ):
     my_dp, me = lax.axis_index("dp"), lax.axis_index("fsdp")
-    chunks, _, own_rows, piece_width = catalog.shape
+    chunks, _, own, _, piece_width = catalog.shape
     per_dev, rank_rows, block_rows = u_rows.shape[1:]
     count_dev, model_width = x.shape
     width = dy.shape[1]
     features, outputs = model_width // fsdp, width // fsdp
     block_group = per_dev * rank_rows
     lanes = fsdp * block_group
-    total_rows = dp * own_rows
-    own = own_rows // rank_rows
+    total_rows = dp * own * rank_rows
     chips = fsdp // cores
     chip, core = me // cores, lax.rem(me, cores)
-    tile_lanes = 384 if piece_width % 384 == 0 else piece_width
+    tile_lanes = lane_tile(piece_width)
+    parts = piece_width // tile_lanes
+    last = chunks - 1
 
     def peer(offset):
         return lax.rem(me + offset, fsdp)
@@ -65,10 +69,24 @@
         pltpu.make_async_copy(dy_hbm, dy, load_sem.at[1]),
         pltpu.make_async_copy(w_ref, frozen.at[me], load_sem.at[2]),
     ]
-    owns = [
-        pltpu.make_async_copy(pieces_ref.at[k], catalog.at[k, my_dp], own_sem.at[k])
-        for k in range(chunks)
-    ]
+    owns = []
+    for k in range(chunks):
+        ranks = pl.ds(k * rank_rows, rank_rows)
+        place = catalog.at[k, my_dp]
+        if outputs % 128 == 0:
+            owns.append((
+                pltpu.make_async_copy(
+                    down_ref.at[:, ranks, :], place.at[:, :, pl.ds(0, features)], own_sem.at[0, k]
+                ),
+                pltpu.make_async_copy(
+                    up_ref.at[:, ranks, :], place.at[:, :, pl.ds(features, outputs)], own_sem.at[1, k]
+                ),
+            ))
+        else:
+            owns.append((pltpu.make_async_copy(down_ref.at[:, ranks, :], place, own_sem.at[0, k]),))
+    for copies in owns:
+        for copy in copies:
+            copy.start()
 
     lane_block = lax.shift_right_logical(
         lax.broadcasted_iota(jnp.int32, (8, lanes), 1), rank_rows.bit_length() - 1
@@ -104,7 +122,7 @@
 
     def s1_copy(k, offset):
         return remote(
-            pieces_ref.at[k], catalog.at[k, my_dp], s1_send.at[k, offset], s1_recv.at[k, offset],
+            catalog.at[k, my_dp], catalog.at[k, my_dp], s1_send.at[k, offset], s1_recv.at[k, offset],
             (partner(my_dp, offset, dp), me),
         )
 
@@ -114,18 +132,26 @@
             p_recv.at[k, offset], (my_dp, peer(offset)),
         )
 
-    def t_copy(k, offset):
-        return remote(
-            outgoing.at[k, peer(offset)], returned.at[k, me], t_send.at[k, offset],
-            t_recv.at[k, offset], (my_dp, peer(offset)),
-        )
-
-    def g_copy(k, offset):
+    def lanes_of(k, part):
+        return pl.ds(0, piece_width) if k < last else pl.ds(part * tile_lanes, tile_lanes)
+
+    def t_copy(k, offset, part=0):
+        sent = lanes_of(k, part)
+        return remote(
+            outgoing.at[k, peer(offset), :, sent], returned.at[k, me, :, sent],
+            t_send.at[k + part, offset], t_recv.at[k + part, offset], (my_dp, peer(offset)),
+        )
+
+    def g_copy(k, offset, part=0):
         other = partner(my_dp, offset, dp)
-        return remote(
-            catalog.at[k, other], sums_in.at[k, my_dp], g_send.at[k, offset], g_recv.at[k, offset],
-            (other, me),
-        )
+        sent = lanes_of(k, part)
+        return remote(
+            catalog.at[k, other, :, :, sent], sums_in.at[k, my_dp, :, :, sent],
+            g_send.at[k + part, offset], g_recv.at[k + part, offset], (other, me),
+        )
+
+    def parts_of(k):
+        return range(parts) if k == last else range(1)
 
     def right_copy(step):
         source = w_ref.at[my_dp] if step == 0 else frozen.at[me - cores * step, my_dp]
@@ -201,8 +227,13 @@
     def _(offset):
         id_copy(offset).start()
 
-    for offset in range(1, dp):
-        s1_copy(0, offset).start()
+    def share_catalog(k):
+        for copy in owns[k]:
+            copy.wait()
+        for offset in range(1, dp):
+            s1_copy(k, offset).start()
+
+    share_catalog(0)
 
     @pl.when(sends_right(0))
     def _():
@@ -213,9 +244,8 @@
         left_copy(0).start()
 
     for k in range(1, chunks):
-        for offset in range(1, dp):
-            s1_copy(k, offset).start()
-    for copy in owns + loads:
+        share_catalog(k)
+    for copy in loads:
         copy.start()
 
     @pl.loop(1, fsdp)
@@ -236,11 +266,10 @@
     pick[...] = hot.T.astype(jnp.bfloat16)
 
     def choose(k):
-        owns[k].wait()
         for offset in range(1, dp):
             s1_copy(k, offset).wait_recv()
         for start in range(0, piece_width, tile_lanes):
-            table = catalog[k, :, :, start : start + tile_lanes].reshape(total_rows, tile_lanes)
+            table = catalog[k, :, :, :, start : start + tile_lanes].reshape(total_rows, tile_lanes)
             chosen = dot(pick[...], table, 1, 0).astype(jnp.bfloat16)
             outgoing[k, :, :, start : start + tile_lanes] = chosen.reshape(
                 fsdp, block_group, tile_lanes
@@ -291,46 +320,56 @@
         @pl.loop(1, fsdp)
         def _(offset):
             terms_of(peer(offset))
-
-            @pl.when(offset > 1)
-            def _():
-                t_copy(k, offset - 1).start()
+            if k < last:
+
+                @pl.when(offset > 1)
+                def _():
+                    t_copy(k, offset - 1).start()
 
         terms_of(me)
-        t_copy(k, fsdp - 1).start()
+        if k < last:
+            t_copy(k, fsdp - 1).start()
+        else:
+            for part in parts_of(k):
+
+                @pl.loop(1, fsdp)
+                def _(offset):
+                    t_copy(k, offset, part).start()
+
         returned[k, me] = outgoing[k, me]
 
-    def combine(k):
+    def combine(k, part=0):
+        if part == 0:
+            for offset in range(1, dp):
+                s1_copy(k, offset).wait_send()
+
         @pl.loop(1, fsdp)
         def _(offset):
-            t_copy(k, offset).wait_recv()
-
-        for start in range(0, piece_width, tile_lanes):
-            terms = returned[k, :, :, start : start + tile_lanes].reshape(lanes, tile_lanes)
+            t_copy(k, offset, part).wait_recv()
+
+        starts = [part * tile_lanes] if k == last else range(0, piece_width, tile_lanes)
+        for start in starts:
+            tile = slice(start, start + tile_lanes)
+            terms = returned[k, :, :, tile].reshape(lanes, tile_lanes)
             added = dot(put[...], terms, 1, 0).astype(jnp.bfloat16)
-            catalog[k, :, :, start : start + tile_lanes] = added.reshape(dp, own_rows, tile_lanes)
+            catalog[k, :, :, :, tile] = added.reshape(dp, own, rank_rows, tile_lanes)
         for offset in range(1, dp):
-            g_copy(k, offset).start()
-        sums_in[k, my_dp] = catalog[k, my_dp]
-
-    def out_copies(k):
-        part = pl.ds(k * rank_rows, rank_rows)
-        return (
-            pltpu.make_async_copy(down_tile.at[k], down_out.at[:, part, :], out_sem.at[0, k]),
-            pltpu.make_async_copy(up_tile.at[k], up_out.at[:, part, :], out_sem.at[1, k]),
-        )
+            g_copy(k, offset, part).start()
+        for start in starts:
+            tile = slice(start, start + tile_lanes)
+            sums_in[k, my_dp, :, :, tile] = catalog[k, my_dp, :, :, tile]
 
     def finish(k):
-        for offset in range(1, dp):
-            g_copy(k, offset).wait_recv()
+        for part in parts_of(k):
+            for offset in range(1, dp):
+                g_copy(k, offset, part).wait_recv()
         added = sums_in[k, 0].astype(jnp.float32)
         for position in range(1, dp):
             added = added + sums_in[k, position].astype(jnp.float32)
         added = adapter_scale * added
-        down_tile[k] = added[:, :features].reshape(own, rank_rows, features)
-        up_tile[k] = added[:, features:].reshape(own, rank_rows, outputs)
-        for copy in out_copies(k):
-            copy.start()
+        ranks = slice(k * rank_rows, (k + 1) * rank_rows)
+        down_out[:, ranks, :] = added[:, :, :features]
+        up_out[:, ranks, :] = added[:, :, features:]
 
     def columns_of_low():
         for block in range(per_dev):
@@ -345,15 +384,10 @@
                         k, index, ranks, features:
                     ]
 
-    def dx_copy(index):
-        slot = lax.rem(index, 2)
-        return pltpu.make_async_copy(dx_tiles.at[slot], dx_out.at[:, column(index)], dx_sem.at[slot])
-
-    def base(first, last):
-        @pl.loop(first, last)
+    def base_values():
+        @pl.loop(0, fsdp)
         def _(index):
-            weight = frozen[index].reshape(features, width)
-            product = dot(x[:, column(index)], weight, 1, 0)
+            product = dot(x[:, column(index)], frozen[index].reshape(features, width), 1, 0)
 
             @pl.when(index == 0)
             def _():
@@ -363,13 +397,10 @@
             def _():
                 total[...] += product
 
-            base_grad = dot(dy[...], weight, 1, 1)
-
-            @pl.when(index >= 2)
-            def _():
-                dx_copy(index - 2).wait()
-
-            slot = lax.rem(index, 2)
+    def base_grads(first, end):
+        @pl.loop(first, end)
+        def _(index):
+            base_grad = dot(dy[...], frozen[index].reshape(features, width), 1, 1)
             for block in range(per_dev):
                 tokens = slice(block * block_rows, (block + 1) * block_rows)
                 ranks = slice(block * rank_rows, (block + 1) * rank_rows)
@@ -377,76 +408,78 @@
                     [arrived[k, index, ranks, :features] for k in range(chunks)], axis=0
                 )
                 pulled = dot(v_cols[block], down, 1, 0).astype(jnp.bfloat16).astype(jnp.float32)
-                dx_tiles[slot, tokens, :] = (base_grad[tokens, :] + adapter_scale * pulled).astype(
-                    jnp.bfloat16
-                )
-            dx_copy(index).start()
-
-    y_copy = pltpu.make_async_copy(y_tile, y_out, load_sem.at[0])
+                mixed = base_grad[tokens, :] + adapter_scale * pulled
+                dx_out[tokens, column(index)] = mixed.astype(jnp.bfloat16)
 
     def last_values():
         for block in range(per_dev):
             tokens = slice(block * block_rows, (block + 1) * block_rows)
             lifted = dot(u_cols[block], up_blocks[block], 1, 0)
             lifted = lifted.astype(jnp.bfloat16).astype(jnp.float32)
-            y_tile[tokens, :] = (total[tokens, :] + adapter_scale * lifted).astype(jnp.bfloat16)
-        y_copy.start()
+            y_out[tokens, :] = (total[tokens, :] + adapter_scale * lifted).astype(jnp.bfloat16)
+
+    def pass_core(step):
+        def give(from_chip):
+            for offset in range(1, dp):
+                w2_copy(from_chip, offset).wait_recv()
+            w3_copy(from_chip).start()
+
+        @pl.when(gets_right(step))
+        def _():
+            give(chip - step - 1)
+
+        @pl.when(gets_left(step))
+        def _():
+            give(chip + step + 1)
 
     hops = chips - 1
-    relayed = 0
+    relay(0)
     choose(0)
-    relay(0)
-    choose(1)
+    spread_shares(0)
     for copy in loads:
         copy.wait()
+    w3_copy(chip).start()
     for index in range(fsdp):
         dy_slices[index] = dy[:, index * outputs : (index + 1) * outputs]
-    for k in range(2, chunks):
-        choose(k)
-    spread_shares(0)
+    choose(1)
     low_rank(0)
     for step in range(1, hops):
         relay(step)
         spread_shares(step)
-    for k in range(1, chunks):
-        low_rank(k)
-        if k >= 2:
-            combine(k - 2)
-    columns_of_low()
-
-    def w2_done(from_chip):
-        @pl.when(from_chip != chip)
-        def _():
-            for offset in range(1, dp):
-                w2_copy(from_chip, offset).wait_recv()
-
-    for from_chip in range(chips):
-        w2_done(from_chip)
-        w3_copy(from_chip).start()
+    choose(2)
+    low_rank(1)
+    pass_core(0)
+    for k in range(3, chunks):
+        choose(k)
+        combine(k - 3)
+        low_rank(k - 1)
+    for step in range(1, hops):
+        pass_core(step)
     for from_chip in range(chips):
         w3_copy(from_chip).wait_recv()
-    base(0, fsdp // 2)
-    combine(chunks - 2)
-    base(fsdp // 2, fsdp)
+    base_values()
+    combine(chunks - 3)
+    low_rank(last)
+    columns_of_low()
+    base_grads(0, fsdp)
     last_values()
-    for k in range(chunks - 2):
+    combine(last - 1)
+    for part in parts_of(last):
+        combine(last, part)
+    for k in range(chunks):
         finish(k)
-    combine(chunks - 1)
-    finish(chunks - 2)
-    finish(chunks - 1)
 
     @pl.loop(1, fsdp)
     def _(offset):
         id_copy(offset).wait_send()
         for k in range(chunks):
-            t_copy(k, offset).wait_send()
+            for part in parts_of(k):
+                t_copy(k, offset, part).wait_send()
 
     for k in range(chunks):
         for offset in range(1, dp):
-            s1_copy(k, offset).wait_send()
-            g_copy(k, offset).wait_send()
-        for copy in out_copies(k):
-            copy.wait()
+            for part in parts_of(k):
+                g_copy(k, offset, part).wait_send()
     for step in range(hops):
 
         @pl.when(sends_right(step))
@@ -465,9 +498,6 @@
                 w2_copy(from_chip, offset).wait_send()
 
         w3_copy(from_chip).wait_send()
-    for index in (fsdp - 2, fsdp - 1):
-        dx_copy(index).wait()
-    y_copy.wait()
 
 
 def body(
@@ -488,11 +518,12 @@
     outputs = adapter_up_weight.shape[2]
     piece_width = features + outputs
     chunks = rank // rows_chunk
+    steps = chunks - 1 + piece_width // lane_tile(piece_width)
     chips = fsdp // cores
     share_rows = frozen_value_weight.shape[0] // dp
-    pieces = jnp.concatenate([adapter_down_weight.transpose(0, 2, 1), adapter_up_weight], axis=2)
-    pieces = pieces.reshape(own, chunks, rows_chunk, piece_width).transpose(1, 0, 2, 3)
-    pieces = pieces.reshape(chunks, own * rows_chunk, piece_width)
+    down, up = adapter_down_weight.transpose(0, 2, 1), adapter_up_weight
+    if outputs % 128:
+        down = jnp.concatenate([down, up], axis=2)
     weight = frozen_value_weight.reshape(dp, share_rows, width)
     block_group = per_dev * rows_chunk
     lanes = fsdp * block_group
@@ -505,11 +536,11 @@
         pltpu.VMEM((count_dev, model_width), bf16),
         pltpu.VMEM((count_dev, width), bf16),
         pltpu.VMEM((fsdp, count_dev, outputs), bf16),
-        pltpu.VMEM((chunks, dp, own * rows_chunk, piece_width), bf16),
+        pltpu.VMEM((chunks, dp, own, rows_chunk, piece_width), bf16),
         pltpu.VMEM((chunks, fsdp, block_group, piece_width), bf16),
         pltpu.VMEM((chunks, fsdp, block_group, piece_width), bf16),
         pltpu.VMEM((chunks, fsdp, block_group, piece_width), bf16),
-        pltpu.VMEM((chunks, dp, own * rows_chunk, piece_width), bf16),
+        pltpu.VMEM((chunks, dp, own, rows_chunk, piece_width), bf16),
         pltpu.VMEM((fsdp, dp, share_rows, width), bf16),
         pltpu.VMEM((fsdp, 8, lanes), jnp.int32),
         pltpu.VMEM((lanes, total_rows), bf16),
@@ -520,40 +551,34 @@
         pltpu.VMEM((per_dev, block_rows, rank), bf16),
         pltpu.VMEM((per_dev, rank, width), bf16),
         pltpu.VMEM((count_dev, width), f32),
-        pltpu.VMEM((2, count_dev, features), bf16),
-        pltpu.VMEM((count_dev, width), bf16),
-        pltpu.VMEM((chunks, own, rows_chunk, features), f32),
-        pltpu.VMEM((chunks, own, rows_chunk, outputs), f32),
         dma((3,)),
-        dma((chunks,)),
+        dma((2, chunks)),
         dma((chunks, dp)), dma((chunks, dp)),
         dma((fsdp,)), dma((fsdp,)),
         dma((chunks, fsdp)), dma((chunks, fsdp)),
-        dma((chunks, fsdp)), dma((chunks, fsdp)),
-        dma((chunks, dp)), dma((chunks, dp)),
+        dma((steps, fsdp)), dma((steps, fsdp)),
+        dma((steps, dp)), dma((steps, dp)),
         dma((chips,)), dma((chips,)),
         dma((chips,)), dma((chips,)),
         dma((chips, dp)), dma((chips, dp)),
         dma((chips,)), dma((chips,)),
-        dma((2,)),
-        dma((2, chunks)),
     ]
     values, input_gradient, grad_down, grad_up = pl.pallas_call(
         functools.partial(kernel, dp, fsdp),
         out_shape=(
-            jax.ShapeDtypeStruct((count_dev, width), bf16),
-            jax.ShapeDtypeStruct((count_dev, model_width), bf16),
-            jax.ShapeDtypeStruct((own, rank, features), f32),
-            jax.ShapeDtypeStruct((own, rank, outputs), f32),
+            pltpu.VMEM((count_dev, width), bf16),
+            pltpu.VMEM((count_dev, model_width), bf16),
+            pltpu.VMEM((own, rank, features), f32),
+            pltpu.VMEM((own, rank, outputs), f32),
         ),
-        in_specs=[scalars, scalars] + [anywhere] * 4,
-        out_specs=(anywhere,) * 4,
+        in_specs=[scalars, scalars] + [anywhere] * 5,
+        out_specs=(pl.BlockSpec(memory_space=pltpu.VMEM),) * 4,
         scratch_shapes=scratch,
         compiler_params=pltpu.CompilerParams(
-            collective_id=0, has_side_effects=True, vmem_limit_bytes=66_000_000
+            collective_id=0, has_side_effects=True, vmem_limit_bytes=54_000_000
         ),
         name="lora",
-    )(adapter_per_block, block_live_count, pieces, weight, tokens, output_gradient)
+    )(adapter_per_block, block_live_count, down, up, weight, tokens, output_gradient)
     return values, input_gradient, grad_down.transpose(0, 2, 1), grad_up
 
 

time: 234 us -> 212 us (0.906)
  Pallas kernels: 219 us -> 205 us
  local copies, waits for them, and re-layouts: 11.5 us -> 5.61 us
    pallas_call x1, Pallas kernels: 219 us -> 205 us  [body(): pl.pallas_call(functools.partial(kernel, dp, fsdp), out_shape=(pltpu.VMEM...]
    unnamed x8 -> x4, local copies, waits for them, and re-layouts: 10.4 us -> 5.61 us
where the time goes in v2:
time: 212 us; the launch traced here: 211 us
  Pallas kernels  205 us (97%)
  local copies, waits for them, and re-layouts  5.61 us (3%)
    pallas_call x1, Pallas kernels, body(): pl.pallas_call(functools.partial(kernel, dp, fsdp), out_shape=(pltpu.VMEM...  205 us
    unnamed x4, local copies, waits for them, and re-layouts  5.61 us

profile of v2, /device:TPU:25, one launch (start us, length us, event | category | flops | bytes accessed | tf_op | source)
XLA Modules:
  0.0 211.4 jit_solution(8878979108756452315)
XLA Ops:
  0.6 205.2 %lora.1 = (bf16[384,1024]{1,0:T(8,128)(2,1)S(1)}, bf16[384,8192]{1,0:T(8,128)(2,1)S(1)}, f32[8,64,1024]{2,1,0:T(8,128)S(1)}, f32[8,64,128]{2,1,0:T(8,128)S(1)}) custom-call(s32[3]{0:T(128)} %ids_ref.1, s32[3]{0:T(128)} %fill_ref.1, bf16[8,64,1024]{2,1,0:T(8,128)(2,1)} %bitcast.5, bf16[8,64,128]{2,1,0:T(8,128)(2,1)} %up_ref.1, bf16[4,256,1024]{2,1,0:T(8,128)(2,1)} %bitcast.4, ...), custom_call_target="tpu_custom_call" | custom-call | tf_op jit(solution)/shard_map/lora/pallas_call | solution.py:566
  205.8 0.9 copy.15
  206.7 0.7 copy.18
  207.4 1.3 copy.17
  208.7 2.7 %copy.16 = bf16[384,8192]{1,0:T(8,128)(2,1)} copy(bf16[384,8192]{1,0:T(8,128)(2,1)S(1)} %get-tuple-element.13) | data formatting | bytes 12582912

commit v3 on v2

--- a/solution.py
+++ b/solution.py
@@ -10,6 +10,7 @@
 adapter_scale = 0.5
 cores = 2
 rows_chunk = 16
+split_chunks = 2
 mesh_ids = pl.DeviceIdType.MESH
 
 
@@ -57,6 +58,7 @@
     tile_lanes = lane_tile(piece_width)
     parts = piece_width // tile_lanes
     last = chunks - 1
+    whole = max(chunks - split_chunks, 0)
 
     def peer(offset):
         return lax.rem(me + offset, fsdp)
@@ -114,32 +116,58 @@
             device_id=device, device_id_type=mesh_ids,
         )
 
+    def wait_group(array, semaphore):
+        pltpu.make_async_copy(array, array, semaphore).wait()
+
+    others, dp_others = pl.ds(0, fsdp - 1), pl.ds(0, dp - 1)
+
+    def id_group():
+        return id_rows.at[others]
+
+    def s1_group(k):
+        return catalog.at[k, dp_others]
+
+    def p_group(k):
+        return arrived.at[k, others]
+
+    def t_group(k, part):
+        return returned.at[k, others, :, lanes_of(k, part)]
+
+    def g_group(k, part):
+        return sums_in.at[k, dp_others, :, :, lanes_of(k, part)]
+
+    def w2_group():
+        return frozen.at[0, dp_others]
+
     def id_copy(offset):
         return remote(
-            id_rows.at[me], id_rows.at[me], id_send.at[offset], id_recv.at[offset],
+            id_rows.at[me], id_rows.at[me], id_send, id_recv,
             (my_dp, peer(offset)),
         )
 
     def s1_copy(k, offset):
         return remote(
-            catalog.at[k, my_dp], catalog.at[k, my_dp], s1_send.at[k, offset], s1_recv.at[k, offset],
+            catalog.at[k, my_dp], catalog.at[k, my_dp], s1_send.at[k], s1_recv.at[k],
             (partner(my_dp, offset, dp), me),
         )
 
     def p_copy(k, offset):
         return remote(
-            outgoing.at[k, peer(offset)], arrived.at[k, me], p_send.at[k, offset],
-            p_recv.at[k, offset], (my_dp, peer(offset)),
+            outgoing.at[k, peer(offset)], arrived.at[k, me], p_send.at[k],
+            p_recv.at[k], (my_dp, peer(offset)),
         )
 
     def lanes_of(k, part):
-        return pl.ds(0, piece_width) if k < last else pl.ds(part * tile_lanes, tile_lanes)
+        return pl.ds(0, piece_width) if k < whole else pl.ds(part * tile_lanes, tile_lanes)
+
+    def slot_of(k, part):
+        return k if k < whole else whole + (k - whole) * parts + part
 
     def t_copy(k, offset, part=0):
         sent = lanes_of(k, part)
         return remote(
             outgoing.at[k, peer(offset), :, sent], returned.at[k, me, :, sent],
-            t_send.at[k + part, offset], t_recv.at[k + part, offset], (my_dp, peer(offset)),
+            t_send.at[slot_of(k, part)], t_recv.at[slot_of(k, part)], (my_dp, peer(offset)),
         )
 
     def g_copy(k, offset, part=0):
@@ -147,11 +175,11 @@
         sent = lanes_of(k, part)
         return remote(
             catalog.at[k, other, :, :, sent], sums_in.at[k, my_dp, :, :, sent],
-            g_send.at[k + part, offset], g_recv.at[k + part, offset], (other, me),
+            g_send.at[slot_of(k, part)], g_recv.at[slot_of(k, part)], (other, me),
         )
 
     def parts_of(k):
-        return range(parts) if k == last else range(1)
+        return range(parts) if k >= whole else range(1)
 
     def right_copy(step):
         source = w_ref.at[my_dp] if step == 0 else frozen.at[me - cores * step, my_dp]
@@ -182,8 +210,8 @@
     def w2_copy(from_chip, offset):
         row = from_chip * cores + core
         return remote(
-            frozen.at[row, my_dp], frozen.at[row, my_dp], w2_send.at[from_chip, offset],
-            w2_recv.at[from_chip, offset], (partner(my_dp, offset, dp), me),
+            frozen.at[row, my_dp], frozen.at[row, my_dp], w2_send.at[from_chip],
+            w2_recv.at[from_chip], (partner(my_dp, offset, dp), me),
         )
 
     def w3_copy(from_chip):
@@ -248,9 +276,7 @@
     for copy in loads:
         copy.start()
 
-    @pl.loop(1, fsdp)
-    def _(offset):
-        id_copy(offset).wait_recv()
+    wait_group(id_group(), id_recv)
 
     numbers = id_rows[0]
     for position in range(1, fsdp):
@@ -266,8 +292,7 @@
     pick[...] = hot.T.astype(jnp.bfloat16)
 
     def choose(k):
-        for offset in range(1, dp):
-            s1_copy(k, offset).wait_recv()
+        wait_group(s1_group(k), s1_recv.at[k])
         for start in range(0, piece_width, tile_lanes):
             table = catalog[k, :, :, :, start : start + tile_lanes].reshape(total_rows, tile_lanes)
             chosen = dot(pick[...], table, 1, 0).astype(jnp.bfloat16)
@@ -281,9 +306,7 @@
             p_copy(k, offset).start()
 
     def low_rank(k):
-        @pl.loop(1, fsdp)
-        def _(offset):
-            p_copy(k, offset).wait_recv()
+        wait_group(p_group(k), p_recv.at[k])
 
         zero = jnp.zeros((rank_rows, block_rows), jnp.float32)
 
@@ -313,23 +336,21 @@
                 outgoing[k, index, ranks, :features] = down.astype(jnp.bfloat16)
                 outgoing[k, index, ranks, features:] = up.astype(jnp.bfloat16)
 
-        @pl.loop(1, fsdp)
-        def _(offset):
-            p_copy(k, offset).wait_send()
+        wait_group(p_group(k), p_send.at[k])
 
         @pl.loop(1, fsdp)
         def _(offset):
             terms_of(peer(offset))
-            if k < last:
+            if k < whole:
 
                 @pl.when(offset > 1)
                 def _():
                     t_copy(k, offset - 1).start()
 
         terms_of(me)
-        if k < last:
+        if k < whole:
             t_copy(k, fsdp - 1).start()
-        else:
+        elif k < last:
             for part in parts_of(k):
 
                 @pl.loop(1, fsdp)
@@ -338,16 +359,21 @@
 
         returned[k, me] = outgoing[k, me]
 
+    def send_last(part):
+        slot = slot_of(last - 1, part)
+        wait_group(t_group(last - 1, part), t_send.at[slot])
+
+        @pl.loop(1, fsdp)
+        def _(offset):
+            t_copy(last, offset, part).start()
+
     def combine(k, part=0):
         if part == 0:
-            for offset in range(1, dp):
-                s1_copy(k, offset).wait_send()
-
-        @pl.loop(1, fsdp)
-        def _(offset):
-            t_copy(k, offset, part).wait_recv()
-
-        starts = [part * tile_lanes] if k == last else range(0, piece_width, tile_lanes)
+            wait_group(s1_group(k), s1_send.at[k])
+
+        wait_group(t_group(k, part), t_recv.at[slot_of(k, part)])
+
+        starts = [part * tile_lanes] if k >= whole else range(0, piece_width, tile_lanes)
         for start in starts:
             tile = slice(start, start + tile_lanes)
             terms = returned[k, :, :, tile].reshape(lanes, tile_lanes)
@@ -361,8 +387,7 @@
 
     def finish(k):
         for part in parts_of(k):
-            for offset in range(1, dp):
-                g_copy(k, offset, part).wait_recv()
+            wait_group(g_group(k, part), g_recv.at[slot_of(k, part)])
         added = sums_in[k, 0].astype(jnp.float32)
         for position in range(1, dp):
             added = added + sums_in[k, position].astype(jnp.float32)
@@ -420,8 +445,7 @@
 
     def pass_core(step):
         def give(from_chip):
-            for offset in range(1, dp):
-                w2_copy(from_chip, offset).wait_recv()
+            wait_group(w2_group(), w2_recv.at[from_chip])
             w3_copy(from_chip).start()
 
         @pl.when(gets_right(step))
@@ -461,43 +485,49 @@
     combine(chunks - 3)
     low_rank(last)
     columns_of_low()
-    base_grads(0, fsdp)
+    order = [(k, part) for k in (last - 1, last) for part in parts_of(k)]
+    count, early = len(order), len(parts_of(last))
+    share = max(fsdp // 4, 1)
+    for position, (k, part) in enumerate(order):
+        if position < early:
+            send_last(part)
+        if position == 0:
+            base_grads(0, share)
+        if position == early:
+            base_grads(share, 2 * share)
+        combine(k, part)
+    base_grads(2 * share, fsdp)
     last_values()
-    combine(last - 1)
-    for part in parts_of(last):
-        combine(last, part)
     for k in range(chunks):
         finish(k)
 
-    @pl.loop(1, fsdp)
-    def _(offset):
-        id_copy(offset).wait_send()
+    def drain():
+        wait_group(id_group(), id_send)
         for k in range(chunks):
             for part in parts_of(k):
-                t_copy(k, offset, part).wait_send()
-
-    for k in range(chunks):
-        for offset in range(1, dp):
-            for part in parts_of(k):
-                g_copy(k, offset, part).wait_send()
-    for step in range(hops):
-
-        @pl.when(sends_right(step))
-        def _():
-            right_copy(step).wait_send()
-
-        @pl.when(sends_left(step))
-        def _():
-            left_copy(step).wait_send()
-
-    for from_chip in range(chips):
-
-        @pl.when(from_chip != chip)
-        def _():
-            for offset in range(1, dp):
-                w2_copy(from_chip, offset).wait_send()
-
-        w3_copy(from_chip).wait_send()
+                slot = slot_of(k, part)
+                if k != last - 1:
+                    wait_group(t_group(k, part), t_send.at[slot])
+                wait_group(g_group(k, part), g_send.at[slot])
+        for step in range(hops):
+
+            @pl.when(sends_right(step))
+            def _():
+                right_copy(step).wait_send()
+
+            @pl.when(sends_left(step))
+            def _():
+                left_copy(step).wait_send()
+
+        for from_chip in range(chips):
+
+            @pl.when(from_chip != chip)
+            def _():
+                wait_group(w2_group(), w2_send.at[from_chip])
+
+            w3_copy(from_chip).wait_send()
+
+    drain()
 
 
 def body(
@@ -518,7 +548,8 @@
     outputs = adapter_up_weight.shape[2]
     piece_width = features + outputs
     chunks = rank // rows_chunk
-    steps = chunks - 1 + piece_width // lane_tile(piece_width)
+    split = min(split_chunks, chunks)
+    steps = chunks - split + split * (piece_width // lane_tile(piece_width))
     chips = fsdp // cores
     share_rows = frozen_value_weight.shape[0] // dp
     down, up = adapter_down_weight.transpose(0, 2, 1), adapter_up_weight
@@ -553,14 +584,14 @@
         pltpu.VMEM((count_dev, width), f32),
         dma((3,)),
         dma((2, chunks)),
-        dma((chunks, dp)), dma((chunks, dp)),
-        dma((fsdp,)), dma((fsdp,)),
-        dma((chunks, fsdp)), dma((chunks, fsdp)),
-        dma((steps, fsdp)), dma((steps, fsdp)),
-        dma((steps, dp)), dma((steps, dp)),
+        dma((chunks,)), dma((chunks,)),
+        dma, dma,
+        dma((chunks,)), dma((chunks,)),
+        dma((steps,)), dma((steps,)),
+        dma((steps,)), dma((steps,)),
+        dma((chips - 1,)), dma((chips - 1,)),
+        dma((chips - 1,)), dma((chips - 1,)),
         dma((chips,)), dma((chips,)),
-        dma((chips,)), dma((chips,)),
-        dma((chips, dp)), dma((chips, dp)),
         dma((chips,)), dma((chips,)),
     ]
     values, input_gradient, grad_down, grad_up = pl.pallas_call(

time: 212 us -> 203 us (0.958)
  Pallas kernels: 205 us -> 197 us
    pallas_call x1, Pallas kernels: 205 us -> 197 us  [body(): pl.pallas_call(functools.partial(kernel, dp, fsdp), out_shape=(pltpu.VMEM...]
where the time goes in v3:
time: 203 us
  Pallas kernels  197 us (97%)
  local copies, waits for them, and re-layouts  5.61 us (3%)
    pallas_call x1, Pallas kernels, body(): pl.pallas_call(functools.partial(kernel, dp, fsdp), out_shape=(pltpu.VMEM...  197 us
    unnamed x4, local copies, waits for them, and re-layouts  5.61 us

profile of v3, /device:TPU:25, one launch (start us, length us, event | category | flops | bytes accessed | tf_op | source)
XLA Modules:
  0.0 203.2 jit_solution(16409435772908219544)
XLA Ops:
  0.6 196.9 %lora.1 = (bf16[384,1024]{1,0:T(8,128)(2,1)S(1)}, bf16[384,8192]{1,0:T(8,128)(2,1)S(1)}, f32[8,64,1024]{2,1,0:T(8,128)S(1)}, f32[8,64,128]{2,1,0:T(8,128)S(1)}) custom-call(s32[3]{0:T(128)} %ids_ref.1, s32[3]{0:T(128)} %fill_ref.1, bf16[8,64,1024]{2,1,0:T(8,128)(2,1)} %bitcast.5, bf16[8,64,128]{2,1,0:T(8,128)(2,1)} %up_ref.1, bf16[4,256,1024]{2,1,0:T(8,128)(2,1)} %bitcast.4, ...), custom_call_target="tpu_custom_call" | custom-call | tf_op jit(solution)/shard_map/lora/pallas_call | solution.py:597
  197.5 0.9 copy.15
  198.4 0.7 copy.18
  199.1 1.3 copy.17
  200.4 2.7 %copy.16 = bf16[384,8192]{1,0:T(8,128)(2,1)} copy(bf16[384,8192]{1,0:T(8,128)(2,1)S(1)} %get-tuple-element.13) | data formatting | bytes 12582912

commit v4 on v3

--- a/solution.py
+++ b/solution.py
@@ -11,6 +11,7 @@
 cores = 2
 rows_chunk = 16
 split_chunks = 2
+cross_chunks = 1
 mesh_ids = pl.DeviceIdType.MESH
 
 
@@ -35,6 +36,10 @@
     return 384 if piece_width % 384 == 0 else piece_width
 
 
+def crossing_chunks(chunks, chips):
+    return min(cross_chunks, chunks - 2) if chips % 2 == 0 else 0
+
+
 def kernel(
     dp, fsdp,
     ids_ref, fill_ref, down_ref, up_ref, w_ref, x_hbm, dy_hbm,
@@ -42,7 +47,8 @@
     x, dy, dy_slices, catalog, outgoing, arrived, returned, sums_in, frozen, id_rows,
     pick, put, u_rows, v_rows, u_cols, v_cols, up_blocks, total,
     load_sem, own_sem, s1_send, s1_recv, id_send, id_recv, p_send, p_recv, t_send, t_recv,
-    g_send, g_recv, right_send, right_recv, left_send, left_recv, w2_send, w2_recv, w3_send, w3_recv,
+    g_send, g_recv, right_send, right_recv, left_send, left_recv, w2_send, w2_recv, relay_recv,
+    x_send, x_recv, c_send, c_recv, crossed, w3_send, w3_recv,
 ):
     my_dp, me = lax.axis_index("dp"), lax.axis_index("fsdp")
     chunks, _, own, _, piece_width = catalog.shape
@@ -57,6 +63,13 @@
     chip, core = me // cores, lax.rem(me, cores)
     tile_lanes = lane_tile(piece_width)
     parts = piece_width // tile_lanes
+    crossing = crossing_chunks(chunks, chips)
+    direct = chunks - crossing
+    half = fsdp // 2
+    first = me // half * half
+    local, across = me - first, lax.rem(me + half, fsdp)
+    two_hops = dp == 4
+    share_half = frozen.shape[2] // 2
     last = chunks - 1
     whole = max(chunks - split_chunks, 0)
 
@@ -128,7 +141,7 @@
         return catalog.at[k, dp_others]
 
     def p_group(k):
-        return arrived.at[k, others]
+        return arrived.at[k, others] if k < direct else arrived.at[k, pl.ds(0, fsdp - 2)]
 
     def t_group(k, part):
         return returned.at[k, others, :, lanes_of(k, part)]
@@ -136,8 +149,8 @@
     def g_group(k, part):
         return sums_in.at[k, dp_others, :, :, lanes_of(k, part)]
 
-    def w2_group():
-        return frozen.at[0, dp_others]
+    def w2_group(shares=dp - 1):
+        return frozen.at[0, pl.ds(0, shares)]
 
     def id_copy(offset):
         return remote(
@@ -162,6 +175,33 @@
 
     def slot_of(k, part):
         return k if k < whole else whole + (k - whole) * parts + part
+
+    def half_copies(k, offset):
+        target = lax.rem(local + offset, half)
+        return [
+            remote(
+                outgoing.at[k, slot * half + target], arrived.at[k, place], p_send.at[k], p_recv.at[k],
+                (my_dp, first + target),
+            )
+            for slot, place in enumerate((me, across))
+        ]
+
+    def cross_copy(k):
+        return remote(
+            catalog.at[k, my_dp], crossed.at[k - direct, my_dp], x_send.at[k - direct],
+            x_recv.at[k - direct], (my_dp, across),
+        )
+
+    def crossed_copy(k, offset):
+        return remote(
+            crossed.at[k - direct, my_dp], crossed.at[k - direct, my_dp], c_send.at[k - direct],
+            c_recv.at[k - direct], (partner(my_dp, offset, dp), me),
+        )
+
+    def spread_crossed(k):
+        cross_copy(k).wait_recv()
+        for offset in range(1, dp):
+            crossed_copy(k, offset).start()
 
     def t_copy(k, offset, part=0):
         sent = lanes_of(k, part)
@@ -240,16 +280,38 @@
             def _():
                 left_copy(step + 1).start()
 
-    def spread_shares(step):
+    def relay_copy(from_chip, source, target, part):
+        row = from_chip * cores + core
+        rows = frozen.at[row, partner(my_dp, source, dp), pl.ds(part * share_half, share_half)]
+        return remote(
+            rows, rows, w2_send.at[from_chip], relay_recv.at[from_chip],
+            (partner(my_dp, target, dp), me),
+        )
+
+    def each_arrived(step, action):
         @pl.when(gets_right(step))
         def _():
-            for offset in range(1, dp):
-                w2_copy(chip - step - 1, offset).start()
+            action(chip - step - 1)
 
         @pl.when(gets_left(step))
         def _():
-            for offset in range(1, dp):
-                w2_copy(chip + step + 1, offset).start()
+            action(chip + step + 1)
+
+    def spread_shares(step):
+        def send(from_chip):
+            for offset in range(1, 3 if two_hops else dp):
+                w2_copy(from_chip, offset).start()
+
+        each_arrived(step, send)
+
+    def relay_shares(step):
+        def send(from_chip):
+            wait_group(w2_group(2), w2_recv.at[from_chip])
+            relay_copy(from_chip, 1, 2, 0).start()
+            relay_copy(from_chip, 2, 1, 1).start()
+
+        if two_hops:
+            each_arrived(step, send)
 
     @pl.loop(1, fsdp)
     def _(offset):
@@ -293,17 +355,35 @@
 
     def choose(k):
         wait_group(s1_group(k), s1_recv.at[k])
-        for start in range(0, piece_width, tile_lanes):
-            table = catalog[k, :, :, :, start : start + tile_lanes].reshape(total_rows, tile_lanes)
-            chosen = dot(pick[...], table, 1, 0).astype(jnp.bfloat16)
-            outgoing[k, :, :, start : start + tile_lanes] = chosen.reshape(
-                fsdp, block_group, tile_lanes
-            )
-        arrived[k, me] = outgoing[k, me]
-
-        @pl.loop(1, fsdp)
-        def _(offset):
-            p_copy(k, offset).start()
+        tables, picked, targets = [catalog.at[k]], pick[...], fsdp
+        if k >= direct:
+            wait_group(s1_group(k), c_recv.at[k - direct])
+            tables.append(crossed.at[k - direct])
+            rows = pl.ds(pl.multiple_of(first * block_group, half * block_group), half * block_group)
+            picked, targets = pick[rows, :], half
+        for slot, table_ref in enumerate(tables):
+            for start in range(0, piece_width, tile_lanes):
+                tile = slice(start, start + tile_lanes)
+                table = table_ref[:, :, :, tile].reshape(total_rows, tile_lanes)
+                chosen = dot(picked, table, 1, 0).astype(jnp.bfloat16)
+                outgoing[k, slot * half : slot * half + targets, :, tile] = chosen.reshape(
+                    targets, block_group, tile_lanes
+                )
+        if k < direct:
+            arrived[k, me] = outgoing[k, me]
+
+            @pl.loop(1, fsdp)
+            def _(offset):
+                p_copy(k, offset).start()
+
+        else:
+            arrived[k, me] = outgoing[k, local]
+            arrived[k, across] = outgoing[k, half + local]
+
+            @pl.loop(1, half)
+            def _(offset):
+                for copy in half_copies(k, offset):
+                    copy.start()
 
     def low_rank(k):
         wait_group(p_group(k), p_recv.at[k])
@@ -350,7 +430,7 @@
         terms_of(me)
         if k < whole:
             t_copy(k, fsdp - 1).start()
-        elif k < last:
+        else:
             for part in parts_of(k):
 
                 @pl.loop(1, fsdp)
@@ -359,17 +439,11 @@
 
         returned[k, me] = outgoing[k, me]
 
-    def send_last(part):
-        slot = slot_of(last - 1, part)
-        wait_group(t_group(last - 1, part), t_send.at[slot])
-
-        @pl.loop(1, fsdp)
-        def _(offset):
-            t_copy(last, offset, part).start()
-
     def combine(k, part=0):
         if part == 0:
             wait_group(s1_group(k), s1_send.at[k])
+            if k >= direct:
+                cross_copy(k).wait_send()
 
         wait_group(t_group(k, part), t_recv.at[slot_of(k, part)])
 
@@ -409,8 +483,8 @@
                         k, index, ranks, features:
                     ]
 
-    def base_values():
-        @pl.loop(0, fsdp)
+    def base_values(first, end):
+        @pl.loop(first, end)
         def _(index):
             product = dot(x[:, column(index)], frozen[index].reshape(features, width), 1, 0)
 
@@ -445,69 +519,80 @@
 
     def pass_core(step):
         def give(from_chip):
-            wait_group(w2_group(), w2_recv.at[from_chip])
+            if two_hops:
+                wait_group(w2_group(1), relay_recv.at[from_chip])
+            else:
+                wait_group(w2_group(), w2_recv.at[from_chip])
             w3_copy(from_chip).start()
 
-        @pl.when(gets_right(step))
-        def _():
-            give(chip - step - 1)
-
-        @pl.when(gets_left(step))
-        def _():
-            give(chip + step + 1)
+        each_arrived(step, give)
 
     hops = chips - 1
     relay(0)
+    for k in range(direct, chunks):
+        cross_copy(k).start()
     choose(0)
-    spread_shares(0)
     for copy in loads:
         copy.wait()
     w3_copy(chip).start()
     for index in range(fsdp):
         dy_slices[index] = dy[:, index * outputs : (index + 1) * outputs]
     choose(1)
+    spread_shares(0)
     low_rank(0)
-    for step in range(1, hops):
+    for k in range(direct, chunks):
+        spread_crossed(k)
+    for step in range(1, min(2, hops)):
         relay(step)
         spread_shares(step)
     choose(2)
     low_rank(1)
-    pass_core(0)
+    relay_shares(0)
     for k in range(3, chunks):
         choose(k)
-        combine(k - 3)
-        low_rank(k - 1)
-    for step in range(1, hops):
+    for step in range(2, hops):
+        relay(step)
+        spread_shares(step)
+    relay_shares(1)
+    for k in range(chunks - 3):
+        combine(k)
+    for step in range(2, hops):
+        relay_shares(step)
+    for k in range(2, last):
+        low_rank(k)
+    for step in range(min(2, hops)):
         pass_core(step)
+    low_rank(last)
+    for step in range(2, hops):
+        pass_core(step)
+    combine(chunks - 3)
+    columns_of_low()
     for from_chip in range(chips):
         w3_copy(from_chip).wait_recv()
-    base_values()
-    combine(chunks - 3)
-    low_rank(last)
-    columns_of_low()
+
     order = [(k, part) for k in (last - 1, last) for part in parts_of(k)]
-    count, early = len(order), len(parts_of(last))
-    share = max(fsdp // 4, 1)
-    for position, (k, part) in enumerate(order):
-        if position < early:
-            send_last(part)
-        if position == 0:
-            base_grads(0, share)
-        if position == early:
-            base_grads(share, 2 * share)
+    middle, quarter = fsdp // 2, fsdp // 4
+    fill = [(base_values, 0, middle), (base_values, middle, fsdp), (base_grads, 0, quarter)]
+    fill += [(base_grads, quarter, middle)]
+    for k, part in order:
+        if fill:
+            work, start, end = fill.pop(0)
+            work(start, end)
         combine(k, part)
-    base_grads(2 * share, fsdp)
+    for work, start, end in fill + [(base_grads, middle, fsdp)]:
+        work(start, end)
     last_values()
     for k in range(chunks):
         finish(k)
 
     def drain():
+        for k in range(direct, chunks):
+            wait_group(s1_group(k), c_send.at[k - direct])
         wait_group(id_group(), id_send)
         for k in range(chunks):
             for part in parts_of(k):
                 slot = slot_of(k, part)
-                if k != last - 1:
-                    wait_group(t_group(k, part), t_send.at[slot])
+                wait_group(t_group(k, part), t_send.at[slot])
                 wait_group(g_group(k, part), g_send.at[slot])
         for step in range(hops):
 
@@ -552,6 +637,7 @@
     steps = chunks - split + split * (piece_width // lane_tile(piece_width))
     chips = fsdp // cores
     share_rows = frozen_value_weight.shape[0] // dp
+    crossing = crossing_chunks(chunks, chips)
     down, up = adapter_down_weight.transpose(0, 2, 1), adapter_up_weight
     if outputs % 128:
         down = jnp.concatenate([down, up], axis=2)
@@ -591,7 +677,10 @@
         dma((steps,)), dma((steps,)),
         dma((chips - 1,)), dma((chips - 1,)),
         dma((chips - 1,)), dma((chips - 1,)),
-        dma((chips,)), dma((chips,)),
+        dma((chips,)), dma((chips,)), dma((chips,)),
+        dma((max(crossing, 1),)), dma((max(crossing, 1),)),
+        dma((max(crossing, 1),)), dma((max(crossing, 1),)),
+        pltpu.VMEM((max(crossing, 1), dp, own, rows_chunk, piece_width), bf16),
         dma((chips,)), dma((chips,)),
     ]
     values, input_gradient, grad_down, grad_up = pl.pallas_call(
@@ -606,7 +695,7 @@
         out_specs=(pl.BlockSpec(memory_space=pltpu.VMEM),) * 4,
         scratch_shapes=scratch,
         compiler_params=pltpu.CompilerParams(
-            collective_id=0, has_side_effects=True, vmem_limit_bytes=54_000_000
+            collective_id=0, has_side_effects=True, vmem_limit_bytes=56_500_000
         ),
         name="lora",
     )(adapter_per_block, block_live_count, down, up, weight, tokens, output_gradient)

time: 203 us -> 198 us (0.975)
  Pallas kernels: 197 us -> 192 us
    pallas_call x1, Pallas kernels: 197 us -> 192 us  [body(): pl.pallas_call(functools.partial(kernel, dp, fsdp), out_shape=(pltpu.VMEM...]
where the time goes in v4:
time: 198 us
  Pallas kernels  192 us (97%)
  local copies, waits for them, and re-layouts  5.61 us (3%)
    pallas_call x1, Pallas kernels, body(): pl.pallas_call(functools.partial(kernel, dp, fsdp), out_shape=(pltpu.VMEM...  192 us
    unnamed x4, local copies, waits for them, and re-layouts  5.61 us

profile of v4, /device:TPU:25, one launch (start us, length us, event | category | flops | bytes accessed | tf_op | source)
XLA Modules:
  0.0 197.9 jit_solution(11063449882047154290)
XLA Ops:
  0.6 191.7 %lora.1 = (bf16[384,1024]{1,0:T(8,128)(2,1)S(1)}, bf16[384,8192]{1,0:T(8,128)(2,1)S(1)}, f32[8,64,1024]{2,1,0:T(8,128)S(1)}, f32[8,64,128]{2,1,0:T(8,128)S(1)}) custom-call(s32[3]{0:T(128)} %ids_ref.1, s32[3]{0:T(128)} %fill_ref.1, bf16[8,64,1024]{2,1,0:T(8,128)(2,1)} %bitcast.5, bf16[8,64,128]{2,1,0:T(8,128)(2,1)} %up_ref.1, bf16[4,256,1024]{2,1,0:T(8,128)(2,1)} %bitcast.4, ...), custom_call_target="tpu_custom_call" | custom-call | tf_op jit(solution)/shard_map/lora/pallas_call | solution.py:686
  192.3 0.9 copy.15
  193.2 0.7 copy.18
  193.9 1.3 copy.17
  195.2 2.7 %copy.16 = bf16[384,8192]{1,0:T(8,128)(2,1)} copy(bf16[384,8192]{1,0:T(8,128)(2,1)S(1)} %get-tuple-element.13) | data formatting | bytes 12582912

commit v5 on v4

--- a/solution.py
+++ b/solution.py
@@ -9,7 +9,7 @@
 
 adapter_scale = 0.5
 cores = 2
-rows_chunk = 16
+chunk_count = 4
 split_chunks = 2
 cross_chunks = 1
 mesh_ids = pl.DeviceIdType.MESH
@@ -538,34 +538,29 @@
     for index in range(fsdp):
         dy_slices[index] = dy[:, index * outputs : (index + 1) * outputs]
     choose(1)
-    spread_shares(0)
-    low_rank(0)
     for k in range(direct, chunks):
         spread_crossed(k)
+    spread_shares(0)
     for step in range(1, min(2, hops)):
         relay(step)
         spread_shares(step)
+    low_rank(0)
     choose(2)
     low_rank(1)
     relay_shares(0)
-    for k in range(3, chunks):
-        choose(k)
+    choose(3)
     for step in range(2, hops):
         relay(step)
         spread_shares(step)
     relay_shares(1)
-    for k in range(chunks - 3):
-        combine(k)
+    combine(0)
     for step in range(2, hops):
         relay_shares(step)
-    for k in range(2, last):
-        low_rank(k)
-    for step in range(min(2, hops)):
+    low_rank(2)
+    for step in range(hops):
         pass_core(step)
-    low_rank(last)
-    for step in range(2, hops):
-        pass_core(step)
-    combine(chunks - 3)
+    low_rank(3)
+    combine(1)
     columns_of_low()
     for from_chip in range(chips):
         w3_copy(from_chip).wait_recv()
@@ -613,6 +608,34 @@
             w3_copy(from_chip).wait_send()
 
     drain()
+
+
+def store_kernel(y, dx, down, up, y_out, dx_out, down_out, up_out, semaphores):
+    pieces = 4
+    rows = dx.shape[0] // pieces
+    copies = []
+    for piece in range(pieces):
+        part = pl.ds(piece * rows, rows)
+        copies.append(pltpu.make_async_copy(dx.at[part], dx_out.at[part], semaphores.at[piece]))
+    for index, (source, target) in enumerate(((down, down_out), (y, y_out), (up, up_out))):
+        copies.append(pltpu.make_async_copy(source, target, semaphores.at[pieces + index]))
+    for copy in copies:
+        copy.start()
+    for copy in copies:
+        copy.wait()
+
+
+def store(results):
+    vmem, anywhere = pl.BlockSpec(memory_space=pltpu.VMEM), pl.BlockSpec(memory_space=pl.ANY)
+    return pl.pallas_call(
+        store_kernel,
+        out_shape=tuple(jax.ShapeDtypeStruct(array.shape, array.dtype) for array in results),
+        in_specs=[vmem] * len(results),
+        out_specs=(anywhere,) * len(results),
+        scratch_shapes=[pltpu.SemaphoreType.DMA((7,))],
+        compiler_params=pltpu.CompilerParams(vmem_limit_bytes=16_000_000),
+        name="store",
+    )(*results)
 
 
 def body(
@@ -632,7 +655,7 @@
     own, features, rank = adapter_down_weight.shape
     outputs = adapter_up_weight.shape[2]
     piece_width = features + outputs
-    chunks = rank // rows_chunk
+    chunks, rows_chunk = chunk_count, rank // chunk_count
     split = min(split_chunks, chunks)
     steps = chunks - split + split * (piece_width // lane_tile(piece_width))
     chips = fsdp // cores
@@ -683,7 +706,7 @@
         pltpu.VMEM((max(crossing, 1), dp, own, rows_chunk, piece_width), bf16),
         dma((chips,)), dma((chips,)),
     ]
-    values, input_gradient, grad_down, grad_up = pl.pallas_call(
+    results = pl.pallas_call(
         functools.partial(kernel, dp, fsdp),
         out_shape=(
             pltpu.VMEM((count_dev, width), bf16),
@@ -699,6 +722,7 @@
         ),
         name="lora",
     )(adapter_per_block, block_live_count, down, up, weight, tokens, output_gradient)
+    values, input_gradient, grad_down, grad_up = store(results)
     return values, input_gradient, grad_down.transpose(0, 2, 1), grad_up
 
 

time: 198 us -> 195 us (0.985)
  local copies, waits for them, and re-layouts: 5.61 us -> 0 us
    unnamed x4 -> x0, local copies, waits for them, and re-layouts: 5.61 us -> none
    pallas_call x0 -> x1, Pallas kernels: none -> 3.66 us  [store(): pl.pallas_call(store_kernel, out_shape=tuple((jax.ShapeDtypeStruct(array....]
    pallas_call x1, Pallas kernels: 192 us -> 190 us  [body(): pl.pallas_call(functools.partial(kernel, dp, fsdp), out_shape=(pltpu.VMEM...]
where the time goes in v5:
time: 195 us; the launch traced here: 194 us
  Pallas kernels  193 us (99%)
    pallas_call x1, Pallas kernels, body(): pl.pallas_call(functools.partial(kernel, dp, fsdp), out_shape=(pltpu.VMEM...  190 us

profile of v5, /device:TPU:25, one launch (start us, length us, event | category | flops | bytes accessed | tf_op | source)
XLA Modules:
  0.0 194.1 jit_solution(13570372561719607652)
XLA Ops:
  0.6 189.6 %lora.1 = (bf16[384,1024]{1,0:T(8,128)(2,1)S(1)}, bf16[384,8192]{1,0:T(8,128)(2,1)S(1)}, f32[8,64,1024]{2,1,0:T(8,128)S(1)}, f32[8,64,128]{2,1,0:T(8,128)S(1)}) custom-call(s32[3]{0:T(128)} %ids_ref.1, s32[3]{0:T(128)} %fill_ref.1, bf16[8,64,1024]{2,1,0:T(8,128)(2,1)} %bitcast.4, bf16[8,64,128]{2,1,0:T(8,128)(2,1)} %up_ref.1, bf16[4,256,1024]{2,1,0:T(8,128)(2,1)} %bitcast.3, ...), custom_call_target="tpu_custom_call" | custom-call | tf_op jit(solution)/shard_map/lora/pallas_call | solution.py:709
  190.2 3.7 %store.1 = (bf16[384,1024]{1,0:T(8,128)(2,1)}, bf16[384,8192]{1,0:T(8,128)(2,1)}, f32[8,64,1024]{2,1,0:T(8,128)}, f32[8,64,128]{2,1,0:T(8,128)}) custom-call(bf16[384,1024]{1,0:T(8,128)(2,1)S(1)} %get-tuple-element.12.y, bf16[384,8192]{1,0:T(8,128)(2,1)S(1)} %get-tuple-element.13.dx, f32[8,64,1024]{2,1,0:T(8,128)S(1)} %get-tuple-element.14.down, ...), custom_call_target="tpu_custom_call" | custom-call | tf_op jit(solution)/shard_map/store/pallas_call | solution.py:630

commit v6 on v5

--- a/solution.py
+++ b/solution.py
@@ -547,8 +547,8 @@
     low_rank(0)
     choose(2)
     low_rank(1)
+    choose(3)
     relay_shares(0)
-    choose(3)
     for step in range(2, hops):
         relay(step)
         spread_shares(step)

time: 195 us -> 195 us (level)
  no operation moved by 1% of the time
where the time goes in v6:
time: 195 us; the launch traced here: 194 us
  Pallas kernels  193 us (99%)
    pallas_call x1, Pallas kernels, body(): pl.pallas_call(functools.partial(kernel, dp, fsdp), out_shape=(pltpu.VMEM...  190 us

profile of v6, /device:TPU:25, one launch (start us, length us, event | category | flops | bytes accessed | tf_op | source)
XLA Modules:
  0.0 194.1 jit_solution(11036912359644500715)
XLA Ops:
  0.6 189.6 %lora.1 = (bf16[384,1024]{1,0:T(8,128)(2,1)S(1)}, bf16[384,8192]{1,0:T(8,128)(2,1)S(1)}, f32[8,64,1024]{2,1,0:T(8,128)S(1)}, f32[8,64,128]{2,1,0:T(8,128)S(1)}) custom-call(s32[3]{0:T(128)} %ids_ref.1, s32[3]{0:T(128)} %fill_ref.1, bf16[8,64,1024]{2,1,0:T(8,128)(2,1)} %bitcast.4, bf16[8,64,128]{2,1,0:T(8,128)(2,1)} %up_ref.1, bf16[4,256,1024]{2,1,0:T(8,128)(2,1)} %bitcast.3, ...), custom_call_target="tpu_custom_call" | custom-call | tf_op jit(solution)/shard_map/lora/pallas_call | solution.py:709
  190.2 3.7 %store.1 = (bf16[384,1024]{1,0:T(8,128)(2,1)}, bf16[384,8192]{1,0:T(8,128)(2,1)}, f32[8,64,1024]{2,1,0:T(8,128)}, f32[8,64,128]{2,1,0:T(8,128)}) custom-call(bf16[384,1024]{1,0:T(8,128)(2,1)S(1)} %get-tuple-element.12.y, bf16[384,8192]{1,0:T(8,128)(2,1)S(1)} %get-tuple-element.13.dx, f32[8,64,1024]{2,1,0:T(8,128)S(1)} %get-tuple-element.14.down, ...), custom_call_target="tpu_custom_call" | custom-call | tf_op jit(solution)/shard_map/store/pallas_call | solution.py:630
